TPU v7x, 256 devices: a whole 4x4x8 slice. The times are simulated.
256 devices in a mesh: gx: 16 (over x, z_hi), gy: 16 (over z_lo, y, core).
Axes of the slice: x: 4, y: 4, z: 8 (z_hi: 4, z_lo: 2; z = z_hi * 2 + z_lo), core: 2. Of those that a mesh axis runs over, the one named last changes fastest.
Arguments:
- tokens: bfloat16 [256, 256, 2, 512], P('gx', 'gy'), may hold values from -6 to 6
- cotangent: bfloat16 [256, 256, 2, 512], P('gx', 'gy'), may hold values from -6 to 6
- gain_x: float32 [512], replicated, may hold values from 0.1 to 1.9
- w_qkv_x: bfloat16 [512, 1536], replicated, may hold values from -5 to 5, as said below
- w_out_x: bfloat16 [512, 512], replicated, may hold values from -0.25 to 0.25
- gain_y: float32 [512], replicated, may hold values from 0.1 to 1.9
- w_qkv_y: bfloat16 [512, 1536], replicated, may hold values from -5 to 5, as said below
- w_out_y: bfloat16 [512, 512], replicated, may hold values from -0.25 to 0.25
- gain_mlp: float32 [512], replicated, may hold values from 0.1 to 1.9
- w_up: bfloat16 [512, 2048], replicated, may hold values from -0.25 to 0.25
- w_down: bfloat16 [2048, 512], replicated, may hold values from -0.125 to 0.125
Outputs:
- grad_tokens: bfloat16 [256, 256, 2, 512], P('gx', 'gy')
Inputs may be any that keep to these rules, and one draw needn't show every extreme that they name: `w_qkv_x`: query, key and value projections side by side. `w_qkv_y`: query, key and value projections side by side.
All inputs are finite; a program needn't handle non-finite values.
Results may differ from a plain program's by a relative error of at most 0.013.
Values may be sent and summed in bfloat16 or wider, within the bound.
A program may use at most 128 MiB of HBM per device.

v0:
```python
from functools import partial

import jax
import jax.numpy as jnp
from jax import lax
from jax.sharding import PartitionSpec as P

D = 512
HEADS = 8


def to_low(tensor):
    return lax.optimization_barrier(tensor.astype(jnp.bfloat16))


def layer_norm(inputs, norm_gain):
    average = jnp.mean(inputs, -1, keepdims=True)
    centred = inputs - average
    variance = jnp.mean(centred * centred, -1, keepdims=True)
    return centred * lax.rsqrt(variance + 1e-05) * norm_gain


def norm_back(inputs, norm_gain, gradient):
    _, pullback = jax.vjp(lambda tensor: layer_norm(tensor, norm_gain), inputs)
    return pullback(gradient)[0]


def project(tensor, weight):
    lead_dims = tensor.shape[:-1]
    flattened = tensor.reshape(-1, tensor.shape[-1])
    result = jnp.dot(flattened, weight, preferred_element_type=jnp.float32)
    return result.reshape(lead_dims + (weight.shape[1],))


def project_back(tensor, weight):
    lead_dims = tensor.shape[:-1]
    flattened = tensor.reshape(-1, tensor.shape[-1])
    result = lax.dot_general(
        flattened, weight, (((1,), (1,)), ((), ())), preferred_element_type=jnp.float32
    )
    return result.reshape(lead_dims + (weight.shape[0],))


def to_xlines(tensor):
    return lax.all_to_all(tensor, "gx", split_axis=1, concat_axis=0, tiled=True)


def from_xlines(tensor):
    return lax.all_to_all(tensor, "gx", split_axis=0, concat_axis=1, tiled=True)


def to_ylines(tensor):
    return lax.all_to_all(tensor, "gy", split_axis=0, concat_axis=1, tiled=True)


def from_ylines(tensor):
    return lax.all_to_all(tensor, "gy", split_axis=1, concat_axis=0, tiled=True)


def heads_of(tensor, which_part):
    lead_dims = tensor.shape[:-1]
    block_part = tensor[..., which_part * D : (which_part + 1) * D]
    return block_part.reshape(lead_dims + (HEADS, D // HEADS))


def softmax_rows(queries, key_part, layout, key_layout):
    scores = jnp.einsum(
        layout + "hd," + key_layout + "hd->bzhqk",
        queries,
        key_part,
        preferred_element_type=jnp.float32,
    )
    scores = scores * (D // HEADS) ** (-0.5)
    highest = jnp.max(scores, -1, keepdims=True)
    exponent = jnp.exp(scores - highest)
    return exponent / jnp.sum(exponent, -1, keepdims=True)


def attend(qkv_proj, layout):
    key_layout = layout.replace("q", "k")
    queries, key_part, value_part = (
        heads_of(qkv_proj, 0),
        heads_of(qkv_proj, 1),
        heads_of(qkv_proj, 2),
    )
    probs_low = softmax_rows(queries, key_part, layout, key_layout).astype(jnp.bfloat16)
    result = jnp.einsum(
        "bzhqk," + key_layout + "hd->" + layout + "hd",
        probs_low,
        value_part,
        preferred_element_type=jnp.float32,
    )
    return result.reshape(qkv_proj.shape[:-1] + (D,)).astype(jnp.bfloat16)


def attend_back(qkv_proj, grad_out, layout):
    key_layout = layout.replace("q", "k")
    scale = (D // HEADS) ** (-0.5)
    queries, key_part, value_part = (
        heads_of(qkv_proj, 0),
        heads_of(qkv_proj, 1),
        heads_of(qkv_proj, 2),
    )
    probs = softmax_rows(queries, key_part, layout, key_layout)
    probs_low = probs.astype(jnp.bfloat16)
    grad_heads = heads_of(grad_out, 0)
    grad_probs = jnp.einsum(
        layout + "hd," + key_layout + "hd->bzhqk",
        grad_heads,
        value_part,
        preferred_element_type=jnp.float32,
    )
    grad_scores = probs * (grad_probs - jnp.sum(probs * grad_probs, -1, keepdims=True))
    grad_low = grad_scores.astype(jnp.bfloat16)
    grad_q = jnp.einsum(
        "bzhqk," + key_layout + "hd->" + layout + "hd",
        grad_low,
        key_part,
        preferred_element_type=jnp.float32,
    )
    grad_k = jnp.einsum(
        "bzhqk," + layout + "hd->" + key_layout + "hd",
        grad_low,
        queries,
        preferred_element_type=jnp.float32,
    )
    grad_v = jnp.einsum(
        "bzhqk," + layout + "hd->" + key_layout + "hd",
        probs_low,
        grad_heads,
        preferred_element_type=jnp.float32,
    )
    lead_dims = qkv_proj.shape[:-1] + (D,)
    return jnp.concatenate(
        [
            (grad_q * scale).astype(jnp.bfloat16).reshape(lead_dims),
            (grad_k * scale).astype(jnp.bfloat16).reshape(lead_dims),
            grad_v.astype(jnp.bfloat16).reshape(lead_dims),
        ],
        -1,
    )


def mix_projected(stream, norm_gain, w_qkv, w_out, to_lines, from_lines, layout):
    stream_f = stream.astype(jnp.float32)
    normed = layer_norm(stream_f, norm_gain).astype(jnp.bfloat16)
    qkv_proj = project(normed, w_qkv).astype(jnp.bfloat16)
    qkv_lines = to_lines(qkv_proj)
    mixed_out = from_lines(attend(qkv_lines, layout))
    updated = to_low(stream_f + project(mixed_out, w_out))
    return (updated, qkv_lines)


def back_projected(
    stream, gradient, qkv_lines, norm_gain, w_qkv, w_out, to_lines, from_lines, layout
):
    grad_mixed = project_back(gradient, w_out).astype(jnp.bfloat16)
    grad_qkv = from_lines(attend_back(qkv_lines, to_lines(grad_mixed), layout))
    grad_normed = project_back(grad_qkv, w_qkv)
    return to_low(
        gradient.astype(jnp.float32) + norm_back(stream.astype(jnp.float32), norm_gain, grad_normed)
    )


def mlp_back(stream, cotangent, gain_mlp, w_up, w_down):
    stream_f = stream.astype(jnp.float32)
    normed = layer_norm(stream_f, gain_mlp).astype(jnp.bfloat16)
    pre_act = project(normed, w_up)
    grad_act = project_back(cotangent, w_down).astype(jnp.bfloat16)
    _, pullback = jax.vjp(partial(jax.nn.gelu, approximate=True), pre_act)
    grad_pre = pullback(grad_act.astype(jnp.float32))[0].astype(jnp.bfloat16)
    return to_low(
        cotangent.astype(jnp.float32) + norm_back(stream_f, gain_mlp, project_back(grad_pre, w_up))
    )


def local(
    tokens, cotangent, gain_x, w_qkv_x, w_out_x, gain_y, w_qkv_y, w_out_y, gain_mlp, w_up, w_down
):
    stream_1, stored_x = mix_projected(
        tokens, gain_x, w_qkv_x, w_out_x, to_xlines, from_xlines, "qbz"
    )
    stream_2, stored_y = mix_projected(
        stream_1, gain_y, w_qkv_y, w_out_y, to_ylines, from_ylines, "bqz"
    )
    grad_2 = mlp_back(stream_2, cotangent, gain_mlp, w_up, w_down)
    grad_1 = back_projected(
        stream_1, grad_2, stored_y, gain_y, w_qkv_y, w_out_y, to_ylines, from_ylines, "bqz"
    )
    grad_tokens = back_projected(
        tokens, grad_1, stored_x, gain_x, w_qkv_x, w_out_x, to_xlines, from_xlines, "qbz"
    )
    return grad_tokens


def solution(mesh):
    in_specs = (
        P("gx", "gy", None, None),
        P("gx", "gy", None, None),
        P(),
        P(),
        P(),
        P(),
        P(),
        P(),
        P(),
        P(),
        P(),
    )
    out_specs = P("gx", "gy", None, None)
    return jax.shard_map(local, mesh=mesh, in_specs=in_specs, out_specs=out_specs, check_vma=False)
```

profile of v0, /device:TPU:40, one launch (start us, length us, event | category | flops | bytes accessed | tf_op | source)
XLA Modules:
  0.0 311.0 jit_solution(9509628758100267012)
XLA Ops:
  2.7 2.6 convolution_convert_fusion.1
  5.4 1.6 copy.65
  7.0 49.8 %all_to_all.102 = bf16[16,16,2,1536]{3,2,0,1:T(2,128)(2,1)S(1)} all-to-all(bf16[16,16,2,1536]{3,2,0,1:T(2,128)(2,1)S(1)} %copy.65), channel_id=1, replica_groups=mesh['gx'=16,'gy'=16] {'gx'}, dimensions={1} | all-to-all | bytes 3145728 | tf_op jit(solution)/shard_map/all_to_all | solution.py:45
  58.3 1.4 copy.68
  59.8 2.2 copy.67
  62.0 3.4 %fusion.135 = (f32[2,8,256]{2,1,0:T(8,128)S(1)}, f32[2,8,256,256]{2,3,1,0:T(8,128)}) fusion(bf16[256,2,8,64]{0,3,2,1:T(8,128)(2,1)S(1)} %bitcast.170, bf16[256,2,8,64]{0,3,2,1:T(8,128)(2,1)S(1)} %bitcast.168), kind=kOutput, calls=%fused_computation.158 | convolution fusion | flops 137363712 | bytes 5259264 | tf_op jit(solution)/shard_map/sub | solution.py:75
  65.5 3.7 %convolution_convert_fusion.8 = bf16[2,8,64,256]{3,2,1,0:T(8,128)(2,1)} fusion(bf16[256,2,8,64]{0,3,2,1:T(8,128)(2,1)} %bitcast.182, f32[2,8,256,256]{2,3,1,0:T(8,128)} %get-tuple-element.12, f32[2,8,256]{2,1,0:T(8,128)S(1)} %get-tuple-element.11), kind=kOutput, calls=%fused_computation.86 | convolution fusion | flops 136577024 | bytes 5259264 | tf_op jit(solution)/shard_map/bzhqk,kbzhd->qbzhd/dot_general | solution.py:87
  70.5 22.9 %all_to_all.103 = bf16[256,1,2,512]{3,2,1,0:T(2,128)(2,1)S(1)} all-to-all(bf16[256,1,2,512]{3,2,1,0:T(2,128)(2,1)S(1)} %copy.71), channel_id=1, replica_groups=mesh['gx'=16,'gy'=16] {'gx'}, dimensions={0} | all-to-all | bytes 1048576 | tf_op jit(solution)/shard_map/all_to_all | solution.py:49
  93.5 1.5 fusion.68
  96.7 24.9 %all_to_all.104 = bf16[16,16,2,1536]{3,1,2,0:T(8,128)(2,1)S(1)} all-to-all(bf16[16,16,2,1536]{3,1,2,0:T(8,128)(2,1)S(1)} %convolution_convert_fusion), channel_id=1, replica_groups=mesh['gx'=16,'gy'=16] {'gy'}, dimensions={0} | all-to-all | bytes 3145728 | tf_op jit(solution)/shard_map/all_to_all | solution.py:53
  122.9 2.0 copy.77
  124.9 2.1 copy.76
  127.0 2.1 copy.75
  129.1 4.7 %fusion.136 = (f32[2,8,256]{2,1,0:T(8,128)S(1)}, f32[2,8,256,256]{2,3,1,0:T(8,128)}) fusion(bf16[256,2,8,64]{0,3,2,1:T(8,128)(2,1)} %bitcast.174, bf16[256,2,8,64]{0,3,2,1:T(8,128)(2,1)} %bitcast.172), kind=kOutput, calls=%fused_computation.159 | convolution fusion | flops 137363712 | bytes 5259264 | tf_op jit(solution)/shard_map/sub | solution.py:75
  133.7 3.7 %convolution_convert_fusion.7 = bf16[2,8,64,256]{3,2,1,0:T(8,128)(2,1)} fusion(bf16[256,2,8,64]{0,3,2,1:T(8,128)(2,1)} %bitcast.184, f32[2,8,256,256]{2,3,1,0:T(8,128)} %get-tuple-element.14, f32[2,8,256]{2,1,0:T(8,128)S(1)} %get-tuple-element.13), kind=kOutput, calls=%fused_computation.85 | convolution fusion | flops 136577024 | bytes 5259264 | tf_op jit(solution)/shard_map/bzhqk,bkzhd->bqzhd/dot_general | solution.py:87
  137.4 2.0 copy.79
  139.4 6.9 %all-to-all-start.3 = ((bf16[1,256,2,512]{3,2,0,1:T(2,128)(2,1)}), bf16[1,256,2,512]{3,2,0,1:T(2,128)(2,1)}, u32[]{:S(2)}, u32[]{:S(2)}) async-start(bf16[1,256,2,512]{3,2,0,1:T(2,128)(2,1)} %copy.79), calls=%async_computation.3 | async-start | bytes 1048576 | tf_op jit(solution)/shard_map/all_to_all | solution.py:57
  146.3 3.7 %convolution_convert_fusion.2 = bf16[16,16,2,2048]{3,1,2,0:T(8,128)(2,1)} fusion(bf16[2048,512]{1,0:T(8,128)(2,1)S(1)} %copy-done, bf16[16,16,2,512]{3,2,1,0:T(2,128)(2,1)} %param.12), kind=kOutput, calls=%fused_computation.28 | convolution fusion | flops 1074790400 | bytes 4718592 | tf_op jit(solution)/shard_map/dot_general | solution.py:38
  150.0 4.4 %all-to-all-done.3 = bf16[1,256,2,512]{3,2,0,1:T(2,128)(2,1)} async-done(((bf16[1,256,2,512]{3,2,0,1:T(2,128)(2,1)}), bf16[1,256,2,512]{3,2,0,1:T(2,128)(2,1)}, u32[]{:S(2)}, u32[]{:S(2)}) %all-to-all-start.3) | async-done | bytes 524320 | tf_op jit(solution)/shard_map/all_to_all | solution.py:57
  154.5 1.6 fusion.69
  156.7 7.0 %fusion.77 = (f32[16,16,2]{1,2,0:T(2,128)S(1)}, f32[16,16,2,512]{3,1,2,0:T(8,128)S(1)}) fusion(bf16[16,16,2,512]{3,1,2,0:T(8,128)(2,1)S(1)} %fusion.69, f32[16,16,2]{1,2,0:T(2,128)S(1)} %broadcast_multiply_fusion, f32[512]{0:T(512)S(1)} %copy-done.20, bf16[512,2048]{1,0:T(8,128)(2,1)} %param.20, bf16[16,16,2,2048]{3,1,2,0:T(8,128)(2,1)} %convolution_convert_fusion.2, ...), kind=kOutput, calls=%fused_computation.94 | convolution fusion | flops 2172124672 | bytes 5775360 | tf_op jit(solution)/shard_map/dot_general | solution.py:38
  166.1 13.4 %all_to_all.105 = bf16[16,16,2,512]{3,1,2,0:T(8,128)(2,1)S(1)} all-to-all(bf16[16,16,2,512]{3,1,2,0:T(8,128)(2,1)S(1)} %convolution_convert_fusion.4), channel_id=1, replica_groups=mesh['gx'=16,'gy'=16] {'gy'}, dimensions={0} | all-to-all | bytes 1048576 | tf_op jit(solution)/shard_map/all_to_all | solution.py:53
  180.7 4.0 %convolution_convert_fusion.6 = bf16[2,8,64,256]{3,2,1,0:T(8,128)(2,1)} fusion(bf16[256,2,8,64]{0,3,2,1:T(8,128)(2,1)S(1)} %copy.83, f32[2,8,256,256]{2,3,1,0:T(8,128)} %get-tuple-element.14, f32[2,8,256]{2,1,0:T(8,128)S(1)} %get-tuple-element.13), kind=kOutput, calls=%fused_computation.84 | convolution fusion | flops 136577024 | bytes 5259264 | tf_op jit(solution)/shard_map/bzhqk,bqzhd->bkzhd/dot_general | solution.py:127
  188.1 2.0 copy.90
  192.5 3.3 %pad_maximum_fusion = bf16[1,256,2,1536]{3,2,0,1:T(2,128)(2,1)S(1)} fusion(bf16[1,256,2,512]{3,2,0,1:T(2,128)(2,1)} %copy.90, bf16[1,256,2,512]{3,2,0,1:T(2,128)(2,1)} %copy.89, bf16[1,256,2,512]{3,2,0,1:T(2,128)(2,1)} %copy.88), kind=kLoop, calls=%fused_computation.38 | loop fusion | flops 4718592 | bytes 3145728 | tf_op jit(solution)/shard_map/concatenate | solution.py:134
  195.8 24.7 %all_to_all.106 = bf16[1,256,2,1536]{3,2,0,1:T(2,128)(2,1)S(1)} all-to-all(bf16[1,256,2,1536]{3,2,0,1:T(2,128)(2,1)S(1)} %pad_maximum_fusion), channel_id=1, replica_groups=mesh['gx'=16,'gy'=16] {'gy'}, dimensions={1} | all-to-all | bytes 3145728 | tf_op jit(solution)/shard_map/all_to_all | solution.py:57
  223.7 21.9 %all_to_all.107 = bf16[16,16,2,512]{3,2,0,1:T(2,128)(2,1)S(1)} all-to-all(bf16[16,16,2,512]{3,2,0,1:T(2,128)(2,1)S(1)} %copy.93), channel_id=1, replica_groups=mesh['gx'=16,'gy'=16] {'gx'}, dimensions={1} | all-to-all | bytes 1048576 | tf_op jit(solution)/shard_map/all_to_all | solution.py:45
  247.1 3.9 %convolution_convert_fusion.5 = bf16[2,8,64,256]{3,2,1,0:T(8,128)(2,1)} fusion(bf16[256,2,8,64]{0,3,2,1:T(8,128)(2,1)S(1)} %copy.95, f32[2,8,256,256]{2,3,1,0:T(8,128)} %get-tuple-element.12, f32[2,8,256]{2,1,0:T(8,128)S(1)} %get-tuple-element.11), kind=kOutput, calls=%fused_computation.83 | convolution fusion | flops 136577024 | bytes 5259264 | tf_op jit(solution)/shard_map/bzhqk,qbzhd->kbzhd/dot_general | solution.py:127
  252.9 1.6 fusion.73
  258.4 2.0 copy.101
  260.4 3.0 pad_maximum_fusion.1
  263.4 44.1 %all_to_all.108 = bf16[256,1,2,1536]{3,2,1,0:T(2,128)(2,1)S(1)} all-to-all(bf16[256,1,2,1536]{3,2,1,0:T(2,128)(2,1)S(1)} %pad_maximum_fusion.1), channel_id=1, replica_groups=mesh['gx'=16,'gy'=16] {'gx'}, dimensions={0} | all-to-all | bytes 3145728 | tf_op jit(solution)/shard_map/all_to_all | solution.py:49
  (99 shorter events, 32.3 us)
Async XLA Ops:
  0.0 146.3 %copy-start = (bf16[2048,512]{1,0:T(8,128)(2,1)S(1)}, bf16[2048,512]{1,0:T(8,128)(2,1)}, u32[]{:S(2)}) copy-start(bf16[2048,512]{1,0:T(8,128)(2,1)} %param.21) | copy-start | bytes 6291460
  58.3 7.1 %copy-start.7 = (bf16[256,1,2,512]{0,3,2,1:T(8,128)(2,1)}, bf16[256,1,2,512]{0,3,2,1:T(8,128)(2,1)S(1)}, u32[]{:S(2)}) copy-start(bf16[256,1,2,512]{0,3,2,1:T(8,128)(2,1)S(1)} %copy.69) | copy-start | bytes 1572868
  59.8 5.7 %copy-start.9 = (bf16[256,1,2,512]{0,3,2,1:T(8,128)(2,1)}, bf16[256,1,2,512]{0,3,2,1:T(8,128)(2,1)S(1)}, u32[]{:S(2)}) copy-start(bf16[256,1,2,512]{0,3,2,1:T(8,128)(2,1)S(1)} %copy.68) | copy-start | bytes 1572868
  65.5 28.0 %copy-start.2 = (bf16[16,16,2,512]{3,2,1,0:T(2,128)(2,1)S(1)}, bf16[16,16,2,512]{3,2,1,0:T(2,128)(2,1)}, u32[]{:S(2)}) copy-start(bf16[16,16,2,512]{3,2,1,0:T(2,128)(2,1)} %param.11) | copy-start | bytes 1572868
  69.2 26.4 %copy-start.21 = (f32[512]{0:T(512)S(1)}, f32[512]{0:T(512)}, u32[]{:S(2)}) copy-start(f32[512]{0:T(512)} %param.16) | copy-start | bytes 6148
  70.5 25.1 %copy-start.17 = (bf16[512,1536]{1,0:T(8,128)(2,1)S(1)}, bf16[512,1536]{1,0:T(8,128)(2,1)}, u32[]{:S(2)}) copy-start(bf16[512,1536]{1,0:T(8,128)(2,1)} %param.17) | copy-start | bytes 4718596
  139.4 15.0 %all-to-all-start.3 = ((bf16[1,256,2,512]{3,2,0,1:T(2,128)(2,1)}), bf16[1,256,2,512]{3,2,0,1:T(2,128)(2,1)}, u32[]{:S(2)}, u32[]{:S(2)}) async-start(bf16[1,256,2,512]{3,2,0,1:T(2,128)(2,1)} %copy.79), calls=%async_computation.3 | async-start | bytes 1048576 | tf_op jit(solution)/shard_map/all_to_all | solution.py:57
  150.0 6.6 %copy-start.20 = (f32[512]{0:T(512)S(1)}, f32[512]{0:T(512)}, u32[]{:S(2)}) copy-start(f32[512]{0:T(512)} %param.19) | copy-start | bytes 6148
  163.7 1.9 copy-start.13
  180.7 4.0 %copy-start.6 = (f32[2,8,256,256]{2,3,1,0:T(8,128)S(1)}, f32[2,8,256,256]{2,3,1,0:T(8,128)}, u32[]{:S(2)}) copy-start(f32[2,8,256,256]{2,3,1,0:T(8,128)} %get-tuple-element.14) | copy-start | bytes 12582916
  180.7 4.0 %copy-start.16 = (bf16[1,256,2,512]{1,3,2,0:T(8,128)(2,1)S(1)}, bf16[1,256,2,512]{1,3,2,0:T(8,128)(2,1)}, u32[]{:S(2)}) copy-start(bf16[1,256,2,512]{1,3,2,0:T(8,128)(2,1)} %copy.75) | copy-start | bytes 1572868
  185.5 1.0 copy-start.12
  186.6 1.0 copy-start.11
  192.5 28.0 %copy-start.18 = (bf16[512,1536]{1,0:T(8,128)(2,1)S(1)}, bf16[512,1536]{1,0:T(8,128)(2,1)}, u32[]{:S(2)}) copy-start(bf16[512,1536]{1,0:T(8,128)(2,1)} %param.17) | copy-start | bytes 4718596
  221.6 1.0 copy-start.14
  222.7 24.4 %copy-start.3 = (bf16[16,16,2,512]{3,1,2,0:T(8,128)(2,1)}, bf16[16,16,2,512]{3,1,2,0:T(8,128)(2,1)S(1)}, u32[]{:S(2)}) copy-start(bf16[16,16,2,512]{3,1,2,0:T(8,128)(2,1)S(1)} %add_convert_fusion.1) | copy-start | bytes 1572868
  247.0 3.9 %copy-start.5 = (f32[2,8,256,256]{2,3,1,0:T(8,128)S(1)}, f32[2,8,256,256]{2,3,1,0:T(8,128)}, u32[]{:S(2)}) copy-start(f32[2,8,256,256]{2,3,1,0:T(8,128)} %get-tuple-element.12) | copy-start | bytes 12582916
  247.0 3.9 %copy-start.15 = (bf16[256,1,2,512]{0,3,2,1:T(8,128)(2,1)S(1)}, bf16[256,1,2,512]{0,3,2,1:T(8,128)(2,1)}, u32[]{:S(2)}) copy-start(bf16[256,1,2,512]{0,3,2,1:T(8,128)(2,1)} %copy.67) | copy-start | bytes 1572868
  251.8 1.0 copy-start.10
  252.9 1.6 copy-start.8
  260.4 47.0 %copy-start.19 = (bf16[512,1536]{1,0:T(8,128)(2,1)S(1)}, bf16[512,1536]{1,0:T(8,128)(2,1)}, u32[]{:S(2)}) copy-start(bf16[512,1536]{1,0:T(8,128)(2,1)} %param.14) | copy-start | bytes 4718596
  260.4 47.0 %copy-start.22 = (f32[512]{0:T(512)S(1)}, f32[512]{0:T(512)}, u32[]{:S(2)}) copy-start(f32[512]{0:T(512)} %param.13) | copy-start | bytes 6148
  307.5 1.8 copy-start.4
  307.5 3.5 %copy-start.1 = (bf16[2048,512]{1,0:T(8,128)(2,1)S(1)}, bf16[2048,512]{1,0:T(8,128)(2,1)}, u32[]{:S(2)}) copy-start(bf16[2048,512]{1,0:T(8,128)(2,1)} %param.21) | copy-start | bytes 6291460
where the time goes:
time: 312 us; the launch traced here: 311 us
  blocking collectives  202 us (65%)
  matrix products  50 us (16%)
  local copies, waits for them, and re-layouts  32 us (10%)
  other arithmetic  15.5 us (5%)
  starting transfers between devices  6.85 us (2%)
  waiting for transfers between devices  4.45 us (1%)
    all_to_all x2, blocking collectives, to_xlines(): return lax.all_to_all(tensor, 'gx', split_axis=1, concat_axis=0, tiled=True)  71.6 us
    all_to_all x2, blocking collectives, from_xlines(): return lax.all_to_all(tensor, 'gx', split_axis=0, concat_axis=1, tiled=True)  67 us
    all_to_all x2, blocking collectives, to_ylines(): return lax.all_to_all(tensor, 'gy', split_axis=0, concat_axis=1, tiled=True)  38.4 us
    all_to_all x1, blocking collectives, from_ylines(): return lax.all_to_all(tensor, 'gy', split_axis=1, concat_axis=0, tiled=True)  24.7 us
    dot_general x6, matrix products, project_back(): lax.dot_general(flattened, weight, (((1,), (1,)), ((), ())), preferred_el...  14 us
    slice x8, local copies, waits for them, and re-layouts, heads_of(): block_part = tensor[..., which_part * D:(which_part + 1) * D]  12.3 us
    sub x2, matrix products, softmax_rows(): exponent = jnp.exp(scores - highest)  8.12 us
    dot_general x2, matrix products, attend_back(): jnp.einsum('bzhqk,' + layout + 'hd->' + key_layout + 'hd', probs_low, gra...  7.87 us
  transfers between devices with their start and end apart: 1, of which 1 were waited for; matrix products, arithmetic and copies ran while one was open for 1% of the time, Pallas kernels for 0%

commit v1 on v0

--- a/solution.py
+++ b/solution.py
@@ -141,21 +141,18 @@
     )
 
 
-def mix_projected(stream, norm_gain, w_qkv, w_out, to_lines, from_lines, layout):
+def mix_lines(stream, norm_gain, w_qkv, w_out, layout):
     stream_f = stream.astype(jnp.float32)
     normed = layer_norm(stream_f, norm_gain).astype(jnp.bfloat16)
-    qkv_proj = project(normed, w_qkv).astype(jnp.bfloat16)
-    qkv_lines = to_lines(qkv_proj)
-    mixed_out = from_lines(attend(qkv_lines, layout))
+    qkv_lines = project(normed, w_qkv).astype(jnp.bfloat16)
+    mixed_out = attend(qkv_lines, layout)
     updated = to_low(stream_f + project(mixed_out, w_out))
     return (updated, qkv_lines)
 
 
-def back_projected(
-    stream, gradient, qkv_lines, norm_gain, w_qkv, w_out, to_lines, from_lines, layout
-):
+def back_lines(stream, gradient, qkv_lines, norm_gain, w_qkv, w_out, layout):
     grad_mixed = project_back(gradient, w_out).astype(jnp.bfloat16)
-    grad_qkv = from_lines(attend_back(qkv_lines, to_lines(grad_mixed), layout))
+    grad_qkv = attend_back(qkv_lines, grad_mixed, layout)
     grad_normed = project_back(grad_qkv, w_qkv)
     return to_low(
         gradient.astype(jnp.float32) + norm_back(stream.astype(jnp.float32), norm_gain, grad_normed)
@@ -177,20 +174,16 @@
 def local(
     tokens, cotangent, gain_x, w_qkv_x, w_out_x, gain_y, w_qkv_y, w_out_y, gain_mlp, w_up, w_down
 ):
-    stream_1, stored_x = mix_projected(
-        tokens, gain_x, w_qkv_x, w_out_x, to_xlines, from_xlines, "qbz"
-    )
-    stream_2, stored_y = mix_projected(
-        stream_1, gain_y, w_qkv_y, w_out_y, to_ylines, from_ylines, "bqz"
-    )
-    grad_2 = mlp_back(stream_2, cotangent, gain_mlp, w_up, w_down)
-    grad_1 = back_projected(
-        stream_1, grad_2, stored_y, gain_y, w_qkv_y, w_out_y, to_ylines, from_ylines, "bqz"
-    )
-    grad_tokens = back_projected(
-        tokens, grad_1, stored_x, gain_x, w_qkv_x, w_out_x, to_xlines, from_xlines, "qbz"
-    )
-    return grad_tokens
+    tokens_x = to_xlines(tokens)
+    cotangent_y = to_ylines(cotangent)
+    stream_1x, qkv_x = mix_lines(tokens_x, gain_x, w_qkv_x, w_out_x, "qbz")
+    stream_1 = to_ylines(from_xlines(stream_1x))
+    stream_2, qkv_y = mix_lines(stream_1, gain_y, w_qkv_y, w_out_y, "bqz")
+    grad_2 = mlp_back(stream_2, cotangent_y, gain_mlp, w_up, w_down)
+    grad_1y = back_lines(stream_1, grad_2, qkv_y, gain_y, w_qkv_y, w_out_y, "bqz")
+    grad_1 = to_xlines(from_ylines(grad_1y))
+    grad_x = back_lines(tokens_x, grad_1, qkv_x, gain_x, w_qkv_x, w_out_x, "qbz")
+    return from_xlines(grad_x)
 
 
 def solution(mesh):

time: 312 us -> 231 us (0.74)
  the two profiles are of different devices: /device:TPU:40 before, /device:TPU:24 now
where the time goes in v1:
time: 231 us; the launch traced here: 229 us
  blocking collectives  108 us (47%)
  matrix products  52.3 us (23%)
  local copies, waits for them, and re-layouts  36.4 us (16%)
  other arithmetic  12.2 us (5%)
  starting transfers between devices  11 us (5%)
  waiting for transfers between devices  9.24 us (4%)
    all_to_all x2, blocking collectives, to_xlines(): return lax.all_to_all(tensor, 'gx', split_axis=1, concat_axis=0, tiled=True)  51.8 us
    all_to_all x2, blocking collectives, from_xlines(): return lax.all_to_all(tensor, 'gx', split_axis=0, concat_axis=1, tiled=True)  42.5 us
    dot_general x6, matrix products, project_back(): lax.dot_general(flattened, weight, (((1,), (1,)), ((), ())), preferred_el...  17 us
    all_to_all x1, blocking collectives, from_ylines(): return lax.all_to_all(tensor, 'gy', split_axis=1, concat_axis=0, tiled=True)  13.5 us
    slice x8, local copies, waits for them, and re-layouts, heads_of(): block_part = tensor[..., which_part * D:(which_part + 1) * D]  12.4 us
    all_to_all x2, starting transfers between devices, to_ylines(): return lax.all_to_all(tensor, 'gy', split_axis=0, concat_axis=1, tiled=True)  11 us
    all_to_all x2, waiting for transfers between devices, to_ylines(): return lax.all_to_all(tensor, 'gy', split_axis=0, concat_axis=1, tiled=True)  9.24 us
    concatenate x6, local copies, waits for them, and re-layouts, attend_back(): jnp.concatenate([(grad_q * scale).astype(jnp.bfloat16).reshape(lead_dims)...  9.1 us
  transfers between devices with their start and end apart: 2, of which 2 were waited for; matrix products, arithmetic and copies ran while one was open for 4% of the time, Pallas kernels for 0%

profile of v1, /device:TPU:24, one launch (start us, length us, event | category | flops | bytes accessed | tf_op | source)
XLA Modules:
  0.0 229.5 jit_solution(3078606832670182966)
XLA Ops:
  0.0 1.7 copy.222
  1.7 29.5 %all_to_all.93 = bf16[16,16,2,512]{3,2,0,1:T(2,128)(2,1)S(1)} all-to-all(bf16[16,16,2,512]{3,2,0,1:T(2,128)(2,1)S(1)} %copy.222), channel_id=1, replica_groups=mesh['gx'=16,'gy'=16] {'gx'}, dimensions={1} | all-to-all | bytes 1048576 | tf_op jit(solution)/shard_map/all_to_all | solution.py:45
  34.0 2.4 %fusion.18 = bf16[256,1,2,1536]{3,0,2,1:T(8,128)(2,1)S(1)} fusion(bf16[512,1536]{1,0:T(8,128)(2,1)} %param.14, f32[256,2,512]{2,0,1:T(8,128)S(1)} %bitcast.211, f32[512]{0:T(512)S(1)} %copy-done.21, f32[256,2]{0,1:T(2,128)S(1)} %rsqrt.36, f32[256,2]{0,1:T(2,128)S(1)} %div.94), kind=kOutput, calls=%fused_computation.29 | convolution fusion | flops 807141376 | bytes 4200448 | tf_op jit(solution)/shard_map/dot_general | solution.py:31
  37.7 2.1 copy.229
  39.8 2.1 copy.228
  41.8 2.0 copy.227
  43.9 4.6 %fusion.127 = (f32[2,8,256]{2,1,0:T(8,128)S(1)}, f32[2,8,256,256]{2,3,1,0:T(8,128)}) fusion(bf16[256,2,8,64]{0,3,2,1:T(8,128)(2,1)} %bitcast.225, bf16[256,2,8,64]{0,3,2,1:T(8,128)(2,1)} %bitcast.223), kind=kOutput, calls=%fused_computation.157 | convolution fusion | flops 137363712 | bytes 5259264 | tf_op jit(solution)/shard_map/sub | solution.py:75
  48.5 2.9 %convolution_convert_fusion.8 = bf16[2,8,64,256]{3,2,1,0:T(8,128)(2,1)S(1)} fusion(bf16[256,2,8,64]{0,3,2,1:T(8,128)(2,1)} %bitcast.237, f32[2,8,256,256]{2,3,1,0:T(8,128)} %get-tuple-element.12, f32[2,8,256]{2,1,0:T(8,128)S(1)} %get-tuple-element.11), kind=kOutput, calls=%fused_computation.79 | convolution fusion | flops 136577024 | bytes 5259264 | tf_op jit(solution)/shard_map/bzhqk,kbzhd->qbzhd/dot_general | solution.py:87
  52.5 21.3 %all_to_all.94 = bf16[256,1,2,512]{3,2,1,0:T(2,128)(2,1)} all-to-all(bf16[256,1,2,512]{3,2,1,0:T(2,128)(2,1)S(1)} %copy.232), channel_id=1, replica_groups=mesh['gx'=16,'gy'=16] {'gx'}, dimensions={0} | all-to-all | bytes 1048576 | tf_op jit(solution)/shard_map/all_to_all | solution.py:49
  73.7 4.7 %all-to-all-start = ((bf16[16,16,2,512]{3,2,1,0:T(2,128)(2,1)}), bf16[16,16,2,512]{3,2,1,0:T(2,128)(2,1)}, u32[]{:S(2)}, u32[]{:S(2)}) async-start(bf16[16,16,2,512]{3,2,1,0:T(2,128)(2,1)} %param.12), calls=%async_computation | async-start | bytes 1048576 | tf_op jit(solution)/shard_map/all_to_all | solution.py:53
  78.4 2.1 copy.285
  80.6 6.6 %all-to-all-done = bf16[16,16,2,512]{3,2,1,0:T(2,128)(2,1)} async-done(((bf16[16,16,2,512]{3,2,1,0:T(2,128)(2,1)}), bf16[16,16,2,512]{3,2,1,0:T(2,128)(2,1)}, u32[]{:S(2)}, u32[]{:S(2)}) %all-to-all-start) | async-done | bytes 524320 | tf_op jit(solution)/shard_map/all_to_all | solution.py:53
  87.1 6.3 %all-to-all-start.3 = ((bf16[16,16,2,512]{3,1,2,0:T(8,128)(2,1)}), bf16[16,16,2,512]{3,1,2,0:T(8,128)(2,1)}, u32[]{:S(2)}, u32[]{:S(2)}) async-start(bf16[16,16,2,512]{3,1,2,0:T(8,128)(2,1)} %bitcast.218), calls=%async_computation.3 | async-start | bytes 1048576 | tf_op jit(solution)/shard_map/all_to_all | solution.py:53
  94.6 2.2 copy.220
  96.8 2.7 %convolution_convert_fusion.2 = bf16[256,2,2048]{2,0,1:T(8,128)(2,1)} fusion(bf16[256,2,512]{2,0,1:T(8,128)(2,1)S(1)} %bitcast.247, bf16[2048,512]{1,0:T(8,128)(2,1)S(1)} %copy-done), kind=kOutput, calls=%fused_computation.28 | convolution fusion | flops 1074790400 | bytes 4718592 | tf_op jit(solution)/shard_map/dot_general | solution.py:38
  99.5 2.7 %all-to-all-done.3 = bf16[16,16,2,512]{3,1,2,0:T(8,128)(2,1)} async-done(((bf16[16,16,2,512]{3,1,2,0:T(8,128)(2,1)}), bf16[16,16,2,512]{3,1,2,0:T(8,128)(2,1)}, u32[]{:S(2)}, u32[]{:S(2)}) %all-to-all-start.3) | async-done | bytes 524320 | tf_op jit(solution)/shard_map/all_to_all | solution.py:53
  106.3 2.4 %fusion.19 = bf16[1,256,2,1536]{3,1,2,0:T(8,128)(2,1)S(1)} fusion(bf16[256,2,512]{2,0,1:T(8,128)(2,1)S(1)} %multiply_convert_fusion.2, bf16[512,1536]{1,0:T(8,128)(2,1)} %param.17), kind=kOutput, calls=%fused_computation.30 | convolution fusion | flops 806092800 | bytes 3670016 | tf_op jit(solution)/shard_map/dot_general | solution.py:31
  111.5 2.3 copy.240
  113.7 3.5 %fusion.128 = (f32[2,8,256]{2,1,0:T(8,128)S(1)}, f32[2,8,256,256]{2,3,1,0:T(8,128)}) fusion(bf16[256,2,8,64]{0,3,2,1:T(8,128)(2,1)S(1)} %bitcast.229, bf16[256,2,8,64]{0,3,2,1:T(8,128)(2,1)S(1)} %bitcast.227), kind=kOutput, calls=%fused_computation.158 | convolution fusion | flops 137363712 | bytes 5259264 | tf_op jit(solution)/shard_map/sub | solution.py:75
  117.2 2.9 %convolution_convert_fusion.7 = bf16[2,8,64,256]{3,2,1,0:T(8,128)(2,1)S(1)} fusion(bf16[256,2,8,64]{0,3,2,1:T(8,128)(2,1)} %bitcast.239, f32[2,8,256,256]{2,3,1,0:T(8,128)} %get-tuple-element.14, f32[2,8,256]{2,1,0:T(8,128)S(1)} %get-tuple-element.13), kind=kOutput, calls=%fused_computation.78 | convolution fusion | flops 136577024 | bytes 5259264 | tf_op jit(solution)/shard_map/bzhqk,bkzhd->bqzhd/dot_general | solution.py:87
  121.1 7.9 %fusion.80 = (f32[256,2]{0,1:T(2,128)S(1)}, f32[256,2,512]{2,0,1:T(8,128)}) fusion(bf16[1,256,2,512]{3,1,2,0:T(8,128)(2,1)S(1)} %fusion.75, f32[256,2]{0,1:T(2,128)S(1)} %broadcast_multiply_fusion.1, f32[512]{0:T(512)S(1)} %copy-done.20, bf16[512,2048]{1,0:T(8,128)(2,1)} %param.20, bf16[256,2,2048]{2,0,1:T(8,128)(2,1)} %convolution_convert_fusion.2, ...), kind=kOutput, calls=%fused_computation.91 | convolution fusion | flops 2172124672 | bytes 5775360 | tf_op jit(solution)/shard_map/dot_general | solution.py:38
  129.0 1.7 fusion.106
  130.7 1.9 fusion.82
  134.2 4.1 %convolution_convert_fusion.6 = bf16[2,8,64,256]{3,2,1,0:T(8,128)(2,1)} fusion(bf16[256,2,8,64]{0,3,2,1:T(8,128)(2,1)} %bitcast.243, f32[2,8,256,256]{2,3,1,0:T(8,128)} %get-tuple-element.14, f32[2,8,256]{2,1,0:T(8,128)S(1)} %get-tuple-element.13), kind=kOutput, calls=%fused_computation.77 | convolution fusion | flops 136577024 | bytes 5259264 | tf_op jit(solution)/shard_map/bzhqk,bqzhd->bkzhd/dot_general | solution.py:127
  144.6 2.0 copy.249
  146.7 2.0 copy.250
  148.7 2.8 %multiply_reduce_fusion.5 = (f32[256,2]{0,1:T(2,128)S(1)}, f32[256,2,512]{2,0,1:T(8,128)S(1)}) fusion(f32[16,16,2,512]{3,1,0,2:T(8,128)S(1)} %copy.234, f32[256,2]{0,1:T(2,128)S(1)} %div.99, f32[512]{0:T(512)S(1)} %copy-done.19, bf16[512,1536]{1,0:T(8,128)(2,1)} %param.17, bf16[256,2,512]{2,0,1:T(8,128)(2,1)S(1)} %copy.251, ...), kind=kOutput, calls=%fused_computation.100 | convolution fusion | flops 811073024 | bytes 5249024 | tf_op jit(solution)/shard_map/dot_general | solution.py:38
  152.9 13.5 %all_to_all.95 = bf16[1,256,2,512]{3,2,0,1:T(2,128)(2,1)S(1)} all-to-all(bf16[1,256,2,512]{3,2,0,1:T(2,128)(2,1)S(1)} %copy.252), channel_id=1, replica_groups=mesh['gx'=16,'gy'=16] {'gy'}, dimensions={1} | all-to-all | bytes 1048576 | tf_op jit(solution)/shard_map/all_to_all | solution.py:57
  166.7 22.4 %all_to_all.96 = bf16[16,16,2,512]{3,0,2,1:T(8,128)(2,1)S(1)} all-to-all(bf16[16,16,2,512]{3,0,2,1:T(8,128)(2,1)S(1)} %copy.253), channel_id=1, replica_groups=mesh['gx'=16,'gy'=16] {'gx'}, dimensions={1} | all-to-all | bytes 1048576 | tf_op jit(solution)/shard_map/all_to_all | solution.py:45
  190.6 3.9 %convolution_convert_fusion.5 = bf16[2,8,64,256]{3,2,1,0:T(8,128)(2,1)} fusion(bf16[256,2,8,64]{0,3,2,1:T(8,128)(2,1)S(1)} %bitcast.245, f32[2,8,256,256]{2,3,1,0:T(8,128)} %get-tuple-element.12, f32[2,8,256]{2,1,0:T(8,128)S(1)} %get-tuple-element.11), kind=kOutput, calls=%fused_computation.76 | convolution fusion | flops 136577024 | bytes 5259264 | tf_op jit(solution)/shard_map/bzhqk,qbzhd->kbzhd/dot_general | solution.py:127
  203.0 2.6 %multiply_reduce_fusion.4 = (f32[256,2]{0,1:T(2,128)S(1)}, f32[256,2,512]{2,0,1:T(8,128)S(1)}) fusion(f32[256,2,512]{2,0,1:T(8,128)S(1)} %bitcast.213, f32[256,2]{0,1:T(2,128)S(1)} %div.94, f32[512]{0:T(512)S(1)} %copy-done.21, bf16[512,1536]{1,0:T(8,128)(2,1)} %param.14, bf16[256,2,512]{2,0,1:T(8,128)(2,1)S(1)} %copy.261, ...), kind=kOutput, calls=%fused_computation.99 | convolution fusion | flops 811073024 | bytes 5249024 | tf_op jit(solution)/shard_map/dot_general | solution.py:38
  207.0 21.2 %all_to_all.97 = bf16[256,1,2,512]{3,2,1,0:T(2,128)(2,1)S(1)} all-to-all(bf16[256,1,2,512]{3,2,1,0:T(2,128)(2,1)S(1)} %copy.262), channel_id=1, replica_groups=mesh['gx'=16,'gy'=16] {'gx'}, dimensions={0} | all-to-all | bytes 1048576 | tf_op jit(solution)/shard_map/all_to_all | solution.py:49
  (109 shorter events, 36.0 us)
Async XLA Ops:
  0.0 96.8 %copy-start = (bf16[2048,512]{1,0:T(8,128)(2,1)S(1)}, bf16[2048,512]{1,0:T(8,128)(2,1)}, u32[]{:S(2)}) copy-start(bf16[2048,512]{1,0:T(8,128)(2,1)} %param.21) | copy-start | bytes 6291460
  0.0 34.0 %copy-start.21 = (f32[512]{0:T(512)S(1)}, f32[512]{0:T(512)}, u32[]{:S(2)}) copy-start(f32[512]{0:T(512)} %param.13) | copy-start | bytes 6148
  48.5 2.9 %copy-start.8 = (bf16[512,512]{1,0:T(8,128)(2,1)S(1)}, bf16[512,512]{1,0:T(8,128)(2,1)}, u32[]{:S(2)}) copy-start(bf16[512,512]{1,0:T(8,128)(2,1)} %param.15) | copy-start | bytes 1572868
  73.7 13.4 %all-to-all-start = ((bf16[16,16,2,512]{3,2,1,0:T(2,128)(2,1)}), bf16[16,16,2,512]{3,2,1,0:T(2,128)(2,1)}, u32[]{:S(2)}, u32[]{:S(2)}) async-start(bf16[16,16,2,512]{3,2,1,0:T(2,128)(2,1)} %param.12), calls=%async_computation | async-start | bytes 1048576 | tf_op jit(solution)/shard_map/all_to_all | solution.py:53
  87.1 15.1 %all-to-all-start.3 = ((bf16[16,16,2,512]{3,1,2,0:T(8,128)(2,1)}), bf16[16,16,2,512]{3,1,2,0:T(8,128)(2,1)}, u32[]{:S(2)}, u32[]{:S(2)}) async-start(bf16[16,16,2,512]{3,1,2,0:T(8,128)(2,1)} %bitcast.218), calls=%async_computation.3 | async-start | bytes 1048576 | tf_op jit(solution)/shard_map/all_to_all | solution.py:53
  96.8 9.3 %copy-start.19 = (f32[512]{0:T(512)S(1)}, f32[512]{0:T(512)}, u32[]{:S(2)}) copy-start(f32[512]{0:T(512)} %param.16) | copy-start | bytes 6148
  110.0 7.2 %copy-start.12 = (bf16[1,256,2,512]{1,3,2,0:T(8,128)(2,1)}, bf16[1,256,2,512]{1,3,2,0:T(8,128)(2,1)S(1)}, u32[]{:S(2)}) copy-start(bf16[1,256,2,512]{1,3,2,0:T(8,128)(2,1)S(1)} %copy.242) | copy-start | bytes 1572868
  111.5 8.7 %copy-start.14 = (bf16[1,256,2,512]{1,3,2,0:T(8,128)(2,1)}, bf16[1,256,2,512]{1,3,2,0:T(8,128)(2,1)S(1)}, u32[]{:S(2)}) copy-start(bf16[1,256,2,512]{1,3,2,0:T(8,128)(2,1)S(1)} %copy.241) | copy-start | bytes 1572868
  117.2 2.9 %copy-start.6 = (bf16[512,512]{1,0:T(8,128)(2,1)S(1)}, bf16[512,512]{1,0:T(8,128)(2,1)}, u32[]{:S(2)}) copy-start(bf16[512,512]{1,0:T(8,128)(2,1)} %param.18) | copy-start | bytes 1572868
  117.2 3.9 %copy-start.20 = (f32[512]{0:T(512)S(1)}, f32[512]{0:T(512)}, u32[]{:S(2)}) copy-start(f32[512]{0:T(512)} %param.19) | copy-start | bytes 6148
  129.0 3.7 %copy-start.7 = (bf16[512,512]{1,0:T(8,128)(2,1)S(1)}, bf16[512,512]{1,0:T(8,128)(2,1)}, u32[]{:S(2)}) copy-start(bf16[512,512]{1,0:T(8,128)(2,1)} %param.18) | copy-start | bytes 1572868
  134.2 4.1 %copy-start.5 = (f32[2,8,256,256]{2,3,1,0:T(8,128)S(1)}, f32[2,8,256,256]{2,3,1,0:T(8,128)}, u32[]{:S(2)}) copy-start(f32[2,8,256,256]{2,3,1,0:T(8,128)} %get-tuple-element.14) | copy-start | bytes 12582916
  134.2 4.1 %copy-start.17 = (bf16[1,256,2,512]{1,3,2,0:T(8,128)(2,1)S(1)}, bf16[1,256,2,512]{1,3,2,0:T(8,128)(2,1)}, u32[]{:S(2)}) copy-start(bf16[1,256,2,512]{1,3,2,0:T(8,128)(2,1)} %copy.240) | copy-start | bytes 1572868
  134.2 4.1 %copy-start.18 = (bf16[256,2,512]{0,2,1:T(8,128)(2,1)S(1)}, bf16[256,2,512]{0,2,1:T(8,128)(2,1)}, u32[]{:S(2)}) copy-start(bf16[256,2,512]{0,2,1:T(8,128)(2,1)} %copy.245) | copy-start | bytes 1572868
  139.4 1.0 copy-start.15
  139.4 2.7 %copy-start.13 = (bf16[1,256,2,512]{1,3,2,0:T(8,128)(2,1)S(1)}, bf16[1,256,2,512]{1,3,2,0:T(8,128)(2,1)}, u32[]{:S(2)}) copy-start(bf16[1,256,2,512]{1,3,2,0:T(8,128)(2,1)} %copy-done.12) | copy-start | bytes 1572868
  152.0 37.9 %copy-start.9 = (bf16[512,512]{1,0:T(8,128)(2,1)S(1)}, bf16[512,512]{1,0:T(8,128)(2,1)}, u32[]{:S(2)}) copy-start(bf16[512,512]{1,0:T(8,128)(2,1)} %param.15) | copy-start | bytes 1572868
  189.1 0.8 copy-start.2
  190.6 3.9 %copy-start.4 = (f32[2,8,256,256]{2,3,1,0:T(8,128)S(1)}, f32[2,8,256,256]{2,3,1,0:T(8,128)}, u32[]{:S(2)}) copy-start(f32[2,8,256,256]{2,3,1,0:T(8,128)} %get-tuple-element.12) | copy-start | bytes 12582916
  190.6 3.9 %copy-start.16 = (bf16[256,1,2,512]{0,3,2,1:T(8,128)(2,1)S(1)}, bf16[256,1,2,512]{0,3,2,1:T(8,128)(2,1)}, u32[]{:S(2)}) copy-start(bf16[256,1,2,512]{0,3,2,1:T(8,128)(2,1)} %copy.227) | copy-start | bytes 1572868
  195.4 1.0 copy-start.11
  195.4 2.6 %copy-start.10 = (bf16[256,1,2,512]{0,3,2,1:T(8,128)(2,1)S(1)}, bf16[256,1,2,512]{0,3,2,1:T(8,128)(2,1)}, u32[]{:S(2)}) copy-start(bf16[256,1,2,512]{0,3,2,1:T(8,128)(2,1)} %copy.229) | copy-start | bytes 1572868
  203.0 3.0 %copy-start.3 = (bf16[16,16,1,2,512]{4,1,0,3,2:T(8,128)(2,1)S(1)}, bf16[16,16,1,2,512]{4,1,0,3,2:T(8,128)(2,1)}, u32[]{:S(2)}) copy-start(bf16[16,16,1,2,512]{4,1,0,3,2:T(8,128)(2,1)} %copy-done.2) | copy-start | bytes 1572868
  205.6 23.9 %copy-start.1 = (bf16[2048,512]{1,0:T(8,128)(2,1)S(1)}, bf16[2048,512]{1,0:T(8,128)(2,1)}, u32[]{:S(2)}) copy-start(bf16[2048,512]{1,0:T(8,128)(2,1)} %param.21) | copy-start | bytes 6291460

commit v2 on v1

v2 whole, which is shorter than its diff:
```python
import jax
import jax.numpy as jnp
from jax import lax
from jax.experimental import pallas as pl
from jax.experimental.pallas import tpu as pltpu
from jax.sharding import PartitionSpec as P

D = 512
HEADS = 8
HD = 64
FF = 2048
N = 256
MESH = pl.DeviceIdType.MESH
BF = jnp.bfloat16
F32 = jnp.float32

TOK, COT, Z2, XY2, XY3, Z3, OUT = 0, 2, 4, 6, 8, 10, 12
N_EX = 14


def nn(a, b):
    return jnp.dot(a, b, preferred_element_type=F32)


def nt(a, b):
    return lax.dot_general(a, b, (((1,), (1,)), ((), ())), preferred_element_type=F32)


def tn(a, b):
    return lax.dot_general(a, b, (((0,), (0,)), ((), ())), preferred_element_type=F32)


def norm_parts(v):
    c = v - jnp.mean(v, 0, keepdims=True)
    r = lax.rsqrt(jnp.mean(c * c, 0, keepdims=True) + 1e-05)
    return c * r, r


def norm_back(v, gain, e):
    xhat, r = norm_parts(v)
    dy = e * gain
    m1 = jnp.mean(dy, 0, keepdims=True)
    m2 = jnp.mean(dy * xhat, 0, keepdims=True)
    return r * (dy - m1 - xhat * m2)


def gelu_slope(x):
    k = 0.7978845608028654
    x2 = x * x
    t = jnp.tanh(k * x * (1.0 + 0.044715 * x2))
    return 0.5 * (1.0 + t) + (0.5 * k) * x * (1.0 - t * t) * (1.0 + 0.134145 * x2)


def kernel(
    tok, cot, gain_x, wqx, wox, gain_y, wqy, woy, gain_m, wup, wdn,
    out,
    wqx_v, wox_v, wqy_v, woy_v, wup_v, wdn_v,
    wqx_t, wox_t, wqy_t, woy_t, wup_t,
    gx_t, gy_t, gm_t, perm_a, perm_b, perm_c,
    xl, cl, s1x, zb, pb, yl, g1y, qb, rb, g1x, gtx,
    xt, s1t, s2t, g2t, ct, qkvx, qkvy, mix, nrm, gmx, gqkv, gpre, px, py,
    wsem, ssem, rsem,
):
    gx = lax.axis_index("gx")
    gy = lax.axis_index("gy")
    X, zh = gx // 4, gx % 4
    zl, Yc = gy // 8, gy % 8
    z = zh * 2 + zl
    d_me = X * 8 + Yc

    def at_z(zz):
        return (X * 4 + zz // 2, (zz % 2) * 8 + Yc)

    def at_d(d):
        return ((d // 8) * 4 + zh, zl * 8 + d % 8)

    def gx_peer(p):
        return lax.rem(gx + p, 16)

    def gy_peer(p):
        return lax.rem(gy + p, 16)

    def z_peer(p):
        return lax.rem(z + p, 8)

    def d_peer(p):
        return lax.rem(d_me + p, 32)

    barrier = pltpu.get_barrier_semaphore()

    def loop(lo, hi, body):
        def step(i, carry):
            body(i)
            return carry

        lax.fori_loop(lo, hi, step, 0)

    def greet(device):
        pl.semaphore_signal(barrier, inc=1, device_id=device, device_id_type=MESH)

    loop(1, 16, lambda p: greet((gx_peer(p), gy)))
    loop(1, 16, lambda p: greet((gx, gy_peer(p))))
    loop(1, 8, lambda p: greet(at_z(z_peer(p))))
    loop(1, 32, lambda p: greet(at_d(d_peer(p))))

    weights = (
        (wqx, wqx_v), (wox, wox_v), (wqy, wqy_v), (woy, woy_v), (wup, wup_v), (wdn, wdn_v)
    )
    loads = [pltpu.make_async_copy(s, d, wsem.at[i]) for i, (s, d) in enumerate(weights)]
    for load in loads:
        load.start()

    pl.semaphore_wait(barrier, 68)

    def put(src, dst, device, k):
        pltpu.make_async_remote_copy(
            src_ref=src, dst_ref=dst, send_sem=ssem.at[k], recv_sem=rsem.at[k],
            device_id=device, device_id_type=MESH,
        ).start()

    def keep(src, dst, k):
        pltpu.make_async_copy(src, dst, rsem.at[k]).start()

    def arrived(k):
        pltpu.make_async_copy(pb.at[0], pb.at[0], rsem.at[k]).wait()

    def sent(k, slabs):
        part = pb.at[0, pl.ds(0, slabs)]
        pltpu.make_async_copy(part, part, ssem.at[k]).wait()

    def send_tok(c):
        dst = xl.at[c, pl.ds(2 * zh, 2), X]
        keep(tok.at[gx, c], dst, TOK + c)

        def body(p):
            q = gx_peer(p)
            put(tok.at[q, c], dst, (q, gy), TOK + c)

        loop(1, 16, body)

    def send_cot(c):
        dst = cl.at[c, gy]
        keep(cot.at[gy, c], dst, COT + c)

        def body(p):
            q = gy_peer(p)
            put(cot.at[q, c], dst, (gx, q), COT + c)

        loop(1, 16, body)

    def send_z(src, dst, c, k):
        keep(src.at[c, z], dst.at[c, z], k + c)

        def body(p):
            q = z_peer(p)
            put(src.at[c, q], dst.at[c, z], at_z(q), k + c)

        loop(1, 8, body)

    def send_d(src, dst, c, k):
        keep(src.at[c, d_me], dst.at[c, d_me], k + c)

        def body(p):
            q = d_peer(p)
            put(src.at[c, q], dst.at[c, d_me], at_d(q), k + c)

        loop(1, 32, body)

    def send_out(c):
        dst = out.at[gx, c]
        keep(gtx.at[c, pl.ds(2 * zh, 2), X], dst, OUT + c)

        def body(p):
            q = gx_peer(p)
            put(gtx.at[c, pl.ds(2 * (q % 4), 2), q // 4], dst, (q, gy), OUT + c)

        loop(1, 16, body)

    send_tok(0)
    send_tok(1)

    for g, gt in ((gain_x, gx_t), (gain_y, gy_t), (gain_m, gm_t)):
        col = jnp.transpose(jnp.broadcast_to(g[...], (128, D)))
        gt[:, :128] = col
        gt[:, 128:] = col
    row = lax.broadcasted_iota(jnp.int32, (N, N), 0)
    colm = lax.broadcasted_iota(jnp.int32, (N, N), 1)
    perm_a[...] = jnp.where(colm == (row % 8) * 32 + row // 8, 1.0, 0.0).astype(BF)
    perm_b[...] = jnp.where(colm == (row % 32) * 8 + row // 32, 1.0, 0.0).astype(BF)
    rX, rY, rh, rl = row // 64, (row // 8) % 8, (row // 2) % 4, row % 2
    perm_c[...] = jnp.where(colm == (rl * 8 + rY) * 16 + rX * 4 + rh, 1.0, 0.0).astype(BF)

    def flip(src, dst, cols):
        def body(i):
            s = pl.multiple_of(i * 256, 256)
            dst[pl.ds(s, 256), :] = jnp.transpose(src[:, pl.ds(s, 256)])

        loop(0, cols // 256, body)

    loads[0].wait()
    flip(wqx_v, wqx_t, 1536)
    loads[1].wait()
    flip(wox_v, wox_t, D)
    loads[2].wait()
    flip(wqy_v, wqy_t, 1536)
    loads[3].wait()
    flip(woy_v, woy_t, D)
    loads[4].wait()
    flip(wup_v, wup_t, FF)
    loads[5].wait()

    def blocks(rows, body, size=256):
        loop(0, rows // size, lambda i: body(pl.ds(pl.multiple_of(i * size, size), size)))

    def forward(src_t, gain_t, wq_t, wo_t, qkv, probs, dst_t):
        xhat, _ = norm_parts(src_t[...].astype(F32))
        nrm[...] = (xhat * gain_t[...]).astype(BF)

        def proj(s):
            qkv[s, :] = nn(wq_t[s, :], nrm[...]).astype(BF)

        blocks(1536, proj)

        def head(h):
            o = pl.multiple_of(h * HD, HD)
            q = qkv[pl.ds(o, HD), :] * 0.125
            k = qkv[pl.ds(o + D, HD), :]
            v = qkv[pl.ds(o + 2 * D, HD), :]
            s = tn(k, q)
            e = jnp.exp(s - jnp.max(s, 0, keepdims=True))
            p = e * (1.0 / jnp.sum(e, 0, keepdims=True))
            probs[h] = p
            mix[pl.ds(o, HD), :] = nn(v, p.astype(BF)).astype(BF)

        loop(0, HEADS, head)

        def fin(s):
            dst_t[s, :] = (src_t[s, :].astype(F32) + nn(wo_t[s, :], mix[...])).astype(BF)

        blocks(D, fin)

    def heads_back(qkv, probs, grad_t, wo):
        def gm(s):
            gmx[s, :] = nn(wo[s, :], grad_t[...]).astype(BF)

        blocks(D, gm)

        def head(h):
            o = pl.multiple_of(h * HD, HD)
            q = qkv[pl.ds(o, HD), :]
            k = qkv[pl.ds(o + D, HD), :]
            v = qkv[pl.ds(o + 2 * D, HD), :]
            g = gmx[pl.ds(o, HD), :]
            p = probs[h]
            dp = tn(v, g)
            ds = (p * (dp - jnp.sum(p * dp, 0, keepdims=True))).astype(BF)
            gqkv[pl.ds(o, HD), :] = (nn(k, ds) * 0.125).astype(BF)
            gqkv[pl.ds(o + D, HD), :] = (nt(q, ds) * 0.125).astype(BF)
            gqkv[pl.ds(o + 2 * D, HD), :] = nt(g, p.astype(BF)).astype(BF)

        loop(0, HEADS, head)

    def finish_back(src_t, grad_t, gain_t, wq):
        e = nn(wq[...], gqkv[...])
        return grad_t[...].astype(F32) + norm_back(src_t[...].astype(F32), gain_t[...], e)

    def rows(buf):
        return buf[...].reshape(N, D)

    def x_fwd(c):
        arrived(TOK + c)
        xt[c] = jnp.transpose(rows(xl.at[c]))
        forward(xt.at[c], gx_t, wqx_t, wox_t, qkvx.at[c], px.at[c], s2t)
        s1x[c] = jnp.transpose(s2t[...]).reshape(8, 32, D)
        send_z(s1x, zb, c, Z2)

    def relay2(c):
        arrived(Z2 + c)
        pb[c] = nn(perm_a[...], rows(zb.at[c])).astype(BF).reshape(32, 8, D)
        send_d(pb, yl, c, XY2)

    def relay3(c):
        arrived(XY3 + c)
        rb[c] = nn(perm_b[...], rows(qb.at[c])).astype(BF).reshape(8, 32, D)
        send_z(rb, g1x, c, Z3)

    def y_fwd(c):
        arrived(XY2 + c)
        s1t[...] = jnp.transpose(rows(yl.at[c]))
        forward(s1t, gy_t, wqy_t, woy_t, qkvy, py, s2t)

    def y_mlp(c):
        arrived(COT + c)
        ct[...] = jnp.transpose(nn(perm_c[...], rows(cl.at[c])).astype(BF))
        xhat, _ = norm_parts(s2t[...].astype(F32))
        nrm[...] = (xhat * gm_t[...]).astype(BF)

        def hidden(s):
            act = nn(wup_t[s, :], nrm[...])
            grad = nn(wdn_v[s, :], ct[...]).astype(BF).astype(F32)
            gpre[s, :] = (grad * gelu_slope(act)).astype(BF)

        blocks(FF, hidden)
        e = nn(wup_v[...], gpre[...])
        g2t[...] = (
            ct[...].astype(F32) + norm_back(s2t[...].astype(F32), gm_t[...], e)
        ).astype(BF)

    def y_bwd(c):
        heads_back(qkvy, py, g2t, woy_v)
        g = finish_back(s1t, g2t, gy_t, wqy_v).astype(BF)
        g1y[c] = jnp.transpose(g).reshape(32, 8, D)
        send_d(g1y, qb, c, XY3)

    def x_bwd(c, between):
        arrived(Z3 + c)
        g2t[...] = jnp.transpose(rows(g1x.at[c]))
        heads_back(qkvx.at[c], px.at[c], g2t, wox_v)
        between()
        g = finish_back(xt.at[c], g2t, gx_t, wqx_v).astype(BF)
        gtx[c] = jnp.transpose(g).reshape(8, 4, 8, D)
        send_out(c)

    x_fwd(0)
    send_cot(0)
    send_cot(1)
    x_fwd(1)
    relay2(0)
    y_fwd(0)
    relay2(1)
    y_mlp(0)
    y_bwd(0)
    y_fwd(1)
    relay3(0)
    y_mlp(1)
    y_bwd(1)
    x_bwd(0, lambda: relay3(1))
    x_bwd(1, lambda: None)

    for c in range(2):
        arrived(OUT + c)
        sent(TOK + c, 30)
        sent(COT + c, 30)
        sent(Z2 + c, 28)
        sent(XY2 + c, 31)
        sent(XY3 + c, 31)
        sent(Z3 + c, 28)
        sent(OUT + c, 30)


def local(
    tokens, cotangent, gain_x, w_qkv_x, w_out_x, gain_y, w_qkv_y, w_out_y, gain_mlp, w_up, w_down
):
    tok = jnp.transpose(tokens, (1, 2, 0, 3)).reshape(16, 2, 2, 8, D)
    cot = jnp.transpose(cotangent, (0, 2, 1, 3))
    any_spec = pl.BlockSpec(memory_space=pl.ANY)
    vm = pl.BlockSpec(memory_space=pltpu.VMEM)
    V = pltpu.VMEM
    scratch = [
        V((D, 1536), BF), V((D, D), BF), V((D, 1536), BF), V((D, D), BF), V((D, FF), BF),
        V((FF, D), BF),
        V((1536, D), BF), V((D, D), BF), V((1536, D), BF), V((D, D), BF), V((FF, D), BF),
        V((D, N), F32), V((D, N), F32), V((D, N), F32),
        V((N, N), BF), V((N, N), BF), V((N, N), BF),
        V((2, 8, 4, 8, D), BF),
        V((2, 16, 16, D), BF),
        V((2, 8, 32, D), BF),
        V((2, 8, 32, D), BF),
        V((2, 32, 8, D), BF),
        V((2, 32, 8, D), BF),
        V((2, 32, 8, D), BF),
        V((2, 32, 8, D), BF),
        V((2, 8, 32, D), BF),
        V((2, 8, 32, D), BF),
        V((2, 8, 4, 8, D), BF),
        V((2, D, N), BF),
        V((D, N), BF), V((D, N), BF), V((D, N), BF), V((D, N), BF),
        V((2, 1536, N), BF), V((1536, N), BF),
        V((D, N), BF), V((D, N), BF), V((D, N), BF),
        V((1536, N), BF), V((FF, N), BF),
        V((2, HEADS, N, N), F32), V((HEADS, N, N), F32),
        pltpu.SemaphoreType.DMA((6,)),
        pltpu.SemaphoreType.DMA((N_EX,)),
        pltpu.SemaphoreType.DMA((N_EX,)),
    ]
    res = pl.pallas_call(
        kernel,
        out_shape=jax.ShapeDtypeStruct((16, 2, 2, 8, D), BF),
        in_specs=[any_spec, any_spec, vm, any_spec, any_spec, vm, any_spec, any_spec, vm,
                  any_spec, any_spec],
        out_specs=any_spec,
        scratch_shapes=scratch,
        compiler_params=pltpu.CompilerParams(
            collective_id=0, has_side_effects=True, vmem_limit_bytes=60 * 1024 * 1024
        ),
        name="axial_grad",
    )(
        tok, cot, gain_x.reshape(1, D), w_qkv_x, w_out_x, gain_y.reshape(1, D), w_qkv_y, w_out_y,
        gain_mlp.reshape(1, D), w_up, w_down,
    )
    return jnp.transpose(res.reshape(16, 2, 16, D), (2, 0, 1, 3))


def solution(mesh):
    in_specs = (P("gx", "gy", None, None), P("gx", "gy", None, None)) + (P(),) * 9
    out_specs = P("gx", "gy", None, None)
    return jax.shard_map(local, mesh=mesh, in_specs=in_specs, out_specs=out_specs, check_vma=False)
```

time: 231 us -> 118 us (0.51)
  the two profiles are of different devices: /device:TPU:24 before, /device:TPU:1 now
where the time goes in v2:
time: 118 us; the launch traced here: 117 us
  Pallas kernels  111 us (94%)
  local copies, waits for them, and re-layouts  6.41 us (5%)
    pallas_call x1, Pallas kernels, local(): pl.pallas_call(kernel, out_shape=jax.ShapeDtypeStruct((16, 2, 2, 8, D), B...  111 us
    reshape x1, local copies, waits for them, and re-layouts, local(): return jnp.transpose(res.reshape(16, 2, 16, D), (2, 0, 1, 3))  2.38 us

profile of v2, /device:TPU:1, one launch (start us, length us, event | category | flops | bytes accessed | tf_op | source)
XLA Modules:
  0.0 117.3 jit_solution(2675471534379085332)
XLA Ops:
  0.0 2.1 %copy.20 = bf16[16,2,16,512]{3,2,1,0:T(8,128)(2,1)} copy(bf16[16,2,16,512]{3,1,0,2:T(2,128)(2,1)} %bitcast.17) | data formatting | bytes 1048576 | tf_op jit(solution)/shard_map/transpose | solution.py:354
  2.1 1.9 %copy.19 = bf16[16,16,2,512]{3,1,2,0:T(8,128)(2,1)} copy(bf16[16,16,2,512]{3,2,1,0:T(2,128)(2,1)} %param.12) | data formatting | bytes 1048576 | tf_op args[1]
  4.0 110.9 %axial_grad.1 = bf16[16,2,2,8,512]{4,3,2,1,0:T(8,128)(2,1)} custom-call(bf16[16,2,2,8,512]{4,3,2,1,0:T(8,128)(2,1)} %bitcast.15, bf16[16,2,16,512]{3,2,1,0:T(8,128)(2,1)} %bitcast.16, f32[1,512]{1,0:T(1,128)} %bitcast.18, bf16[512,1536]{1,0:T(8,128)(2,1)} %wqx.1, bf16[512,512]{1,0:T(8,128)(2,1)} %wox.1, f32[1,512]{1,0:T(1,128)} %bitcast.19, ...), custom_call_target="tpu_custom_call" | custom-call | tf_op jit(solution)/shard_map/axial_grad/pallas_call | solution.py:386
  115.0 2.4 %copy.18 = bf16[16,2,16,512]{3,1,0,2:T(2,128)(2,1)} copy(bf16[16,2,16,512]{3,2,1,0:T(8,128)(2,1)} %bitcast.14) | data formatting | bytes 1048576 | tf_op jit(solution)/shard_map/reshape | solution.py:401

commit v3 on v2

v3 whole, which is shorter than its diff:
```python
import jax
import jax.numpy as jnp
from jax import lax
from jax.experimental import pallas as pl
from jax.experimental.pallas import tpu as pltpu
from jax.sharding import PartitionSpec as P

D = 512
HEADS = 8
HD = 64
FF = 2048
N = 256
MESH = pl.DeviceIdType.MESH
BF = jnp.bfloat16
F32 = jnp.float32

TOK, COT, XY, YX, OUT = 0, 2, 4, 6, 8
N_EX = 10


def nn(a, b):
    return jnp.dot(a, b, preferred_element_type=F32)


def nt(a, b):
    return lax.dot_general(a, b, (((1,), (1,)), ((), ())), preferred_element_type=F32)


def tn(a, b):
    return lax.dot_general(a, b, (((0,), (0,)), ((), ())), preferred_element_type=F32)


def norm_parts(v):
    c = v - jnp.mean(v, 0, keepdims=True)
    r = lax.rsqrt(jnp.mean(c * c, 0, keepdims=True) + 1e-05)
    return c * r, r


def norm_back(v, gain, e):
    xhat, r = norm_parts(v)
    dy = e * gain
    m1 = jnp.mean(dy, 0, keepdims=True)
    m2 = jnp.mean(dy * xhat, 0, keepdims=True)
    return r * (dy - m1 - xhat * m2)


def gelu_slope(x):
    k = 0.7978845608028654
    x2 = x * x
    t = jnp.tanh(k * x * (1.0 + 0.044715 * x2))
    return 0.5 * (1.0 + t) + (0.5 * k) * x * (1.0 - t * t) * (1.0 + 0.134145 * x2)


def kernel(
    tok, cot, gain_x, wqx, wox, gain_y, wqy, woy, gain_m, wup, wdn,
    out,
    wqx_v, wox_v, wqy_v, woy_v, wup_v, wdn_v,
    wqx_t, wox_t, wqy_t, woy_t, wup_t,
    gx_t, gy_t, gm_t,
    raw_t, raw_c, tokr, cotr, xl, cl, s1r, yl, g1r, g1x, gtx,
    xt, s1t, s2t, g2t, ct, ga, qkvx, qkvy, mixx, mixy, nrm, gmx, gqkv, gpre, ex, ey, ix, iy,
    rsem_raw, wsem, ssem, rsem,
):
    gx = lax.axis_index("gx")
    gy = lax.axis_index("gy")
    x_me = gx * 16 + gy
    y_me = gy * 16 + gx

    barrier = pltpu.get_barrier_semaphore()

    def loop(lo, hi, body):
        def step(i, carry):
            body(i)
            return carry

        lax.fori_loop(lo, hi, step, 0)

    gx_peers = [lax.rem(gx + p, 16) for p in range(16)]
    gy_peers = [lax.rem(gy + p, 16) for p in range(16)]

    for p in range(1, 16):
        for device in ((gx_peers[p], gy), (gx, gy_peers[p])):
            pl.semaphore_signal(barrier, inc=1, device_id=device, device_id_type=MESH)

    raws = [
        pltpu.make_async_copy(tok, raw_t, rsem_raw.at[0]),
        pltpu.make_async_copy(cot, raw_c, rsem_raw.at[1]),
    ]
    weights = (
        (wqx, wqx_v), (wox, wox_v), (wqy, wqy_v), (woy, woy_v), (wup, wup_v), (wdn, wdn_v)
    )
    loads = [pltpu.make_async_copy(s, d, wsem.at[i]) for i, (s, d) in enumerate(weights)]
    for load in raws + loads:
        load.start()

    def put(src, dst, device, k):
        pltpu.make_async_remote_copy(
            src_ref=src, dst_ref=dst, send_sem=ssem.at[k], recv_sem=rsem.at[k],
            device_id=device, device_id_type=MESH,
        ).start()

    def keep(src, dst, k):
        pltpu.make_async_copy(src, dst, rsem.at[k]).start()

    def arrived(k):
        pltpu.make_async_copy(yl.at[0], yl.at[0], rsem.at[k]).wait()

    def sent(k, tokens):
        part = yl.at[0, pl.ds(0, tokens)]
        pltpu.make_async_copy(part, part, ssem.at[k]).wait()

    def send_tok(c):
        dst = xl.at[c, gx]
        keep(tokr.at[c, gx], dst, TOK + c)
        for q in gx_peers[1:]:
            put(tokr.at[c, q], dst, (q, gy), TOK + c)

    def send_cot(c):
        dst = cl.at[c, gy]
        keep(cotr.at[c, gy], dst, COT + c)
        for q in gy_peers[1:]:
            put(cotr.at[c, q], dst, (gx, q), COT + c)

    def send_out(c):
        dst = out.at[gx, c]
        keep(gtx.at[c, gx], dst, OUT + c)
        for q in gx_peers[1:]:
            put(gtx.at[c, q], dst, (q, gy), OUT + c)

    def send_all(src, dst, row, me, k, c):
        keep(src.at[c, row(gx, gy)], dst.at[c, me], k + c)
        for q in gy_peers[1:]:
            put(src.at[c, row(gx, q)], dst.at[c, me], (gx, q), k + c)

        def body(i):
            a = lax.rem(gx + i, 16)
            for q in gy_peers:
                put(src.at[c, row(a, q)], dst.at[c, me], (a, q), k + c)

        loop(1, 16, body)

    def send_xy(c):
        send_all(s1r, yl, lambda a, b: a * 16 + b, y_me, XY, c)

    def send_yx(c):
        send_all(g1r, g1x, lambda a, b: b * 16 + a, x_me, YX, c)

    def split(raw, dst, swap):
        r = lax.broadcasted_iota(jnp.int32, (N, D), 0)
        s = lax.broadcasted_iota(jnp.int32, (N, D), 1)
        at = (r % 16) * 16 + r // 16 if swap else r
        whole = raw[...].reshape(D, D)
        for c in range(2):
            pick = jnp.where(s == at * 2 + c, 1.0, 0.0).astype(BF)
            dst[c] = nn(pick, whole).astype(BF).reshape(16, 16, D)

    def flip(src, dst, cols):
        def body(i):
            s = pl.multiple_of(i * 256, 256)
            dst[pl.ds(s, 256), :] = jnp.transpose(src[:, pl.ds(s, 256)])

        loop(0, cols // 256, body)

    raws[0].wait()
    split(raw_t, tokr, True)
    raws[1].wait()
    split(raw_c, cotr, False)
    for g, gt in ((gain_x, gx_t), (gain_y, gy_t), (gain_m, gm_t)):
        col = jnp.transpose(jnp.broadcast_to(g[...], (128, D)))
        gt[:, :128] = col
        gt[:, 128:] = col
    loads[0].wait()
    flip(wqx_v, wqx_t, 1536)
    loads[1].wait()
    flip(wox_v, wox_t, D)

    pl.semaphore_wait(barrier, 30)
    send_tok(0)
    send_tok(1)
    send_cot(0)
    send_cot(1)

    loads[2].wait()
    flip(wqy_v, wqy_t, 1536)
    loads[3].wait()
    flip(woy_v, woy_t, D)
    loads[4].wait()
    flip(wup_v, wup_t, FF)
    loads[5].wait()

    def forward(src_t, gain_t, wq_t, wo_t, qkv, es, invs, mix, dst_t):
        xhat, _ = norm_parts(src_t[...].astype(F32))
        nrm[...] = (xhat * gain_t[...]).astype(BF)
        qkv[...] = nn(wq_t[...], nrm[...]).astype(BF)
        for h in range(HEADS):
            o = h * HD
            q = qkv[o : o + HD, :] * 0.125
            k = qkv[o + D : o + D + HD, :]
            v = qkv[o + 2 * D : o + 2 * D + HD, :]
            s = tn(k, q)
            e = jnp.exp(s - jnp.max(s, 0, keepdims=True))
            inv = 1.0 / jnp.sum(e, 0, keepdims=True)
            e = e.astype(BF)
            es[h] = e
            invs[h] = inv
            mix[o : o + HD, :] = (nn(v, e) * inv).astype(BF)
        dst_t[...] = (src_t[...].astype(F32) + nn(wo_t[...], mix[...])).astype(BF)

    def heads_back(qkv, es, invs, mix, grad_t, wo):
        gmx[...] = nn(wo[...], grad_t[...]).astype(BF)
        for h in range(HEADS):
            o = h * HD
            q = qkv[o : o + HD, :]
            k = qkv[o + D : o + D + HD, :]
            v = qkv[o + 2 * D : o + 2 * D + HD, :]
            inv = invs[h]
            gi = gmx[o : o + HD, :].astype(F32) * inv
            delta = jnp.sum(gi * mix[o : o + HD, :].astype(F32), 0, keepdims=True)
            gi = gi.astype(BF)
            e = es[h]
            ds = (e.astype(F32) * (tn(v, gi) - delta)).astype(BF)
            gqkv[o : o + HD, :] = (nn(k, ds) * 0.125).astype(BF)
            gqkv[o + D : o + D + HD, :] = (nt(q, ds) * 0.125).astype(BF)
            gqkv[o + 2 * D : o + 2 * D + HD, :] = nt(gi, e).astype(BF)

    def finish_back(src_t, grad_t, gain_t, wq):
        e = nn(wq[...], gqkv[...])
        return grad_t[...].astype(F32) + norm_back(src_t[...].astype(F32), gain_t[...], e)

    def x_fwd(c):
        arrived(TOK + c)
        xt[c] = jnp.transpose(xl[c].reshape(N, D))
        forward(xt.at[c], gx_t, wqx_t, wox_t, qkvx.at[c], ex.at[c], ix.at[c], mixx.at[c], s2t)
        s1r[c] = jnp.transpose(s2t[...]).reshape(N, 4, 128)
        send_xy(c)

    def y_act(c):
        arrived(COT + c)
        ct[c] = jnp.transpose(cl[c].reshape(N, D))
        ga[c] = nn(wdn_v[...], ct[c]).astype(BF)

    def y_fwd(c):
        arrived(XY + c)
        s1t[...] = jnp.transpose(yl[c].reshape(N, D))
        forward(s1t, gy_t, wqy_t, woy_t, qkvy, ey, iy, mixy, s2t)

    def y_mlp(c):
        xhat, _ = norm_parts(s2t[...].astype(F32))
        nrm[...] = (xhat * gm_t[...]).astype(BF)
        gpre[...] = (
            ga[c].astype(F32) * gelu_slope(nn(wup_t[...], nrm[...]))
        ).astype(BF)
        e = nn(wup_v[...], gpre[...])
        g2t[...] = (
            ct[c].astype(F32) + norm_back(s2t[...].astype(F32), gm_t[...], e)
        ).astype(BF)

    def y_bwd(c):
        heads_back(qkvy, ey, iy, mixy, g2t, woy_v)
        g = finish_back(s1t, g2t, gy_t, wqy_v).astype(BF)
        g1r[c] = jnp.transpose(g).reshape(N, 4, 128)
        send_yx(c)

    def x_bwd(c):
        arrived(YX + c)
        g2t[...] = jnp.transpose(g1x[c].reshape(N, D))
        heads_back(qkvx.at[c], ex.at[c], ix.at[c], mixx.at[c], g2t, wox_v)
        g = finish_back(xt.at[c], g2t, gx_t, wqx_v).astype(BF)
        gtx[c] = jnp.transpose(g).reshape(16, 16, D)
        send_out(c)

    x_fwd(0)
    x_fwd(1)
    y_act(0)
    y_act(1)
    y_fwd(0)
    y_mlp(0)
    y_bwd(0)
    y_fwd(1)
    y_mlp(1)
    y_bwd(1)
    x_bwd(0)
    x_bwd(1)

    for c in range(2):
        arrived(OUT + c)
        sent(TOK + c, 240)
        sent(COT + c, 240)
        sent(XY + c, 255)
        sent(YX + c, 255)
        sent(OUT + c, 240)


def local(
    tokens, cotangent, gain_x, w_qkv_x, w_out_x, gain_y, w_qkv_y, w_out_y, gain_mlp, w_up, w_down
):
    any_spec = pl.BlockSpec(memory_space=pl.ANY)
    vm = pl.BlockSpec(memory_space=pltpu.VMEM)
    V = pltpu.VMEM
    scratch = [
        V((D, 1536), BF), V((D, D), BF), V((D, 1536), BF), V((D, D), BF), V((D, FF), BF),
        V((FF, D), BF),
        V((1536, D), BF), V((D, D), BF), V((1536, D), BF), V((D, D), BF), V((FF, D), BF),
        V((D, N), F32), V((D, N), F32), V((D, N), F32),
        V((16, 16, 2, D), BF), V((16, 16, 2, D), BF),
        V((2, 16, 16, D), BF), V((2, 16, 16, D), BF),
        V((2, 16, 16, D), BF), V((2, 16, 16, D), BF),
        V((2, N, 4, 128), BF), V((2, N, 4, 128), BF),
        V((2, N, 4, 128), BF), V((2, N, 4, 128), BF),
        V((2, 16, 16, D), BF),
        V((2, D, N), BF),
        V((D, N), BF), V((D, N), BF), V((D, N), BF),
        V((2, D, N), BF), V((2, FF, N), BF),
        V((2, 1536, N), BF), V((1536, N), BF),
        V((2, D, N), BF), V((D, N), BF), V((D, N), BF), V((D, N), BF),
        V((1536, N), BF), V((FF, N), BF),
        V((2, HEADS, N, N), BF), V((HEADS, N, N), BF),
        V((2, HEADS, 1, N), F32), V((HEADS, 1, N), F32),
        pltpu.SemaphoreType.DMA((2,)),
        pltpu.SemaphoreType.DMA((6,)),
        pltpu.SemaphoreType.DMA((N_EX,)),
        pltpu.SemaphoreType.DMA((N_EX,)),
    ]
    res = pl.pallas_call(
        kernel,
        out_shape=jax.ShapeDtypeStruct((16, 2, 16, D), BF),
        in_specs=[any_spec, any_spec, vm, any_spec, any_spec, vm, any_spec, any_spec, vm,
                  any_spec, any_spec],
        out_specs=any_spec,
        scratch_shapes=scratch,
        compiler_params=pltpu.CompilerParams(
            collective_id=0, has_side_effects=True, vmem_limit_bytes=60 * 1024 * 1024
        ),
        name="axial_grad",
    )(
        tokens, cotangent, gain_x.reshape(1, D), w_qkv_x, w_out_x, gain_y.reshape(1, D), w_qkv_y,
        w_out_y, gain_mlp.reshape(1, D), w_up, w_down,
    )
    return jnp.transpose(res, (2, 0, 1, 3))


def solution(mesh):
    in_specs = (P("gx", "gy", None, None), P("gx", "gy", None, None)) + (P(),) * 9
    out_specs = P("gx", "gy", None, None)
    return jax.shard_map(local, mesh=mesh, in_specs=in_specs, out_specs=out_specs, check_vma=False)
```

time: 118 us -> 90.5 us (0.77)
  Pallas kernels: 111 us -> 87.9 us
  local copies, waits for them, and re-layouts: 6.41 us -> 2.38 us
    pallas_call x1, Pallas kernels: 111 us -> 87.9 us  [local(): pl.pallas_call(kernel, out_shape=jax.ShapeDtypeStruct((16, 2, 16, D), BF)...]
    reshape x1 -> x0, local copies, waits for them, and re-layouts: 2.38 us -> none  [local(): return jnp.transpose(res.reshape(16, 2, 16, D), (2, 0, 1, 3))]
    unnamed x1 -> x0, local copies, waits for them, and re-layouts: 1.91 us -> none
where the time goes in v3:
time: 90.5 us; the launch traced here: 90.3 us
  Pallas kernels  87.9 us (97%)
  local copies, waits for them, and re-layouts  2.38 us (3%)
    pallas_call x1, Pallas kernels, local(): pl.pallas_call(kernel, out_shape=jax.ShapeDtypeStruct((16, 2, 16, D), BF)...  87.9 us
    transpose x1, local copies, waits for them, and re-layouts, local(): return jnp.transpose(res, (2, 0, 1, 3))  2.38 us

profile of v3, /device:TPU:1, one launch (start us, length us, event | category | flops | bytes accessed | tf_op | source)
XLA Modules:
  0.0 90.3 jit_solution(3448926499025081592)
XLA Ops:
  0.0 87.9 %axial_grad.1 = bf16[16,2,16,512]{3,2,1,0:T(8,128)(2,1)} custom-call(bf16[16,16,2,512]{3,2,1,0:T(2,128)(2,1)} %tok.1, bf16[16,16,2,512]{3,2,1,0:T(2,128)(2,1)} %cot.1, f32[1,512]{1,0:T(1,128)} %bitcast.5, bf16[512,1536]{1,0:T(8,128)(2,1)} %wqx.1, bf16[512,512]{1,0:T(8,128)(2,1)} %wox.1, f32[1,512]{1,0:T(1,128)} %bitcast.6, bf16[512,1536]{1,0:T(8,128)(2,1)} %wqy.1, ...), custom_call_target="tpu_custom_call" | custom-call | tf_op jit(solution)/shard_map/axial_grad/pallas_call | solution.py:324
  87.9 2.4 %copy.12 = bf16[16,16,2,512]{3,2,1,0:T(2,128)(2,1)} copy(bf16[16,16,2,512]{3,0,2,1:T(8,128)(2,1)} %bitcast.4) | data formatting | bytes 1048576 | tf_op jit(solution)/shard_map/transpose | solution.py:339

commit v4 on v3

--- a/solution.py
+++ b/solution.py
@@ -56,15 +56,19 @@
     out,
     wqx_v, wox_v, wqy_v, woy_v, wup_v, wdn_v,
     wqx_t, wox_t, wqy_t, woy_t, wup_t,
-    gx_t, gy_t, gm_t,
+    gx_t, gy_t, gm_t, gain_v,
     raw_t, raw_c, tokr, cotr, xl, cl, s1r, yl, g1r, g1x, gtx,
     xt, s1t, s2t, g2t, ct, ga, qkvx, qkvy, mixx, mixy, nrm, gmx, gqkv, gpre, ex, ey, ix, iy,
     rsem_raw, wsem, ssem, rsem,
 ):
     gx = lax.axis_index("gx")
     gy = lax.axis_index("gy")
+    gyo = lax.rem(gy + 8, 16)
     x_me = gx * 16 + gy
-    y_me = gy * 16 + gx
+    y_me = gyo * 16 + gx
+    X, zh = gx // 4, lax.rem(gx, 4)
+    zl, Yc = gy // 8, lax.rem(gy, 8)
+    z = zh * 2 + zl
 
     barrier = pltpu.get_barrier_semaphore()
 
@@ -75,16 +79,25 @@
 
         lax.fori_loop(lo, hi, step, 0)
 
-    gx_peers = [lax.rem(gx + p, 16) for p in range(16)]
-    gy_peers = [lax.rem(gy + p, 16) for p in range(16)]
-
-    for p in range(1, 16):
-        for device in ((gx_peers[p], gy), (gx, gy_peers[p])):
-            pl.semaphore_signal(barrier, inc=1, device_id=device, device_id_type=MESH)
+    row_peers = [
+        lax.rem(X + dx, 4) * 4 + lax.rem(zh + zl + dz, 4) for dz in (1, 2, 3, 0) for dx in (2, 1, 3, 0)
+    ]
+    near = [
+        lax.rem(Yc // 2 + dy, 4) * 2 + lax.rem(Yc + dc, 2) for dy in (2, 1, 3, 0) for dc in (1, 0)
+    ]
+    gy_peers = [lax.rem(zl + dl, 2) * 8 + q for dl in (1, 0) for q in near]
+
+    for q in row_peers:
+        pl.semaphore_signal(barrier, inc=1, device_id=(q, gyo), device_id_type=MESH)
+    for q in gy_peers[:-1]:
+        pl.semaphore_signal(barrier, inc=1, device_id=(gx, q), device_id_type=MESH)
 
     raws = [
         pltpu.make_async_copy(tok, raw_t, rsem_raw.at[0]),
         pltpu.make_async_copy(cot, raw_c, rsem_raw.at[1]),
+        pltpu.make_async_copy(gain_x, gain_v.at[0], rsem_raw.at[2]),
+        pltpu.make_async_copy(gain_y, gain_v.at[1], rsem_raw.at[3]),
+        pltpu.make_async_copy(gain_m, gain_v.at[2], rsem_raw.at[4]),
     ]
     weights = (
         (wqx, wqx_v), (wox, wox_v), (wqy, wqy_v), (woy, woy_v), (wup, wup_v), (wdn, wdn_v)
@@ -110,40 +123,40 @@
         pltpu.make_async_copy(part, part, ssem.at[k]).wait()
 
     def send_tok(c):
-        dst = xl.at[c, gx]
-        keep(tokr.at[c, gx], dst, TOK + c)
-        for q in gx_peers[1:]:
-            put(tokr.at[c, q], dst, (q, gy), TOK + c)
+        for q in row_peers:
+            put(tokr.at[c, q], xl.at[c, gx], (q, gyo), TOK + c)
 
     def send_cot(c):
         dst = cl.at[c, gy]
         keep(cotr.at[c, gy], dst, COT + c)
-        for q in gy_peers[1:]:
+        for q in gy_peers[:-1]:
             put(cotr.at[c, q], dst, (gx, q), COT + c)
 
     def send_out(c):
-        dst = out.at[gx, c]
-        keep(gtx.at[c, gx], dst, OUT + c)
-        for q in gx_peers[1:]:
-            put(gtx.at[c, q], dst, (q, gy), OUT + c)
+        for q in row_peers:
+            put(gtx.at[c, q], out.at[gx, c], (q, gyo), OUT + c)
+
+    def outward(k, half):
+        return half + jnp.where(k % 2 == 0, k // 2, -((k + 1) // 2))
 
     def send_all(src, dst, row, me, k, c):
         keep(src.at[c, row(gx, gy)], dst.at[c, me], k + c)
-        for q in gy_peers[1:]:
-            put(src.at[c, row(gx, q)], dst.at[c, me], (gx, q), k + c)
-
-        def body(i):
-            a = lax.rem(gx + i, 16)
-            for q in gy_peers:
-                put(src.at[c, row(a, q)], dst.at[c, me], (a, q), k + c)
-
-        loop(1, 16, body)
+
+        def body(i, last=0):
+            zz = lax.rem(z + outward(i // 4, 4), 8)
+            a = lax.rem(X + outward(i % 4, 2), 4) * 4 + zz // 2
+            b = (zz % 2) * 8
+            for q in near[: 8 - last]:
+                put(src.at[c, row(a, b + q)], dst.at[c, me], (a, b + q), k + c)
+
+        loop(0, 31, body)
+        body(31, 1)
 
     def send_xy(c):
         send_all(s1r, yl, lambda a, b: a * 16 + b, y_me, XY, c)
 
     def send_yx(c):
-        send_all(g1r, g1x, lambda a, b: b * 16 + a, x_me, YX, c)
+        send_all(g1r, g1x, lambda a, b: lax.rem(b + 8, 16) * 16 + a, x_me, YX, c)
 
     def split(raw, dst, swap):
         r = lax.broadcasted_iota(jnp.int32, (N, D), 0)
@@ -165,8 +178,9 @@
     split(raw_t, tokr, True)
     raws[1].wait()
     split(raw_c, cotr, False)
-    for g, gt in ((gain_x, gx_t), (gain_y, gy_t), (gain_m, gm_t)):
-        col = jnp.transpose(jnp.broadcast_to(g[...], (128, D)))
+    for i, gt in enumerate((gx_t, gy_t, gm_t)):
+        raws[2 + i].wait()
+        col = jnp.transpose(jnp.broadcast_to(gain_v[i], (128, D)))
         gt[:, :128] = col
         gt[:, 128:] = col
     loads[0].wait()
@@ -174,11 +188,10 @@
     loads[1].wait()
     flip(wox_v, wox_t, D)
 
-    pl.semaphore_wait(barrier, 30)
+    pl.semaphore_wait(barrier, 31)
     send_tok(0)
+    send_cot(0)
     send_tok(1)
-    send_cot(0)
-    send_cot(1)
 
     loads[2].wait()
     flip(wqy_v, wqy_t, 1536)
@@ -270,6 +283,7 @@
         send_out(c)
 
     x_fwd(0)
+    send_cot(1)
     x_fwd(1)
     y_act(0)
     y_act(1)
@@ -284,24 +298,23 @@
 
     for c in range(2):
         arrived(OUT + c)
-        sent(TOK + c, 240)
+        sent(TOK + c, 256)
         sent(COT + c, 240)
         sent(XY + c, 255)
         sent(YX + c, 255)
-        sent(OUT + c, 240)
+        sent(OUT + c, 256)
 
 
 def local(
     tokens, cotangent, gain_x, w_qkv_x, w_out_x, gain_y, w_qkv_y, w_out_y, gain_mlp, w_up, w_down
 ):
     any_spec = pl.BlockSpec(memory_space=pl.ANY)
-    vm = pl.BlockSpec(memory_space=pltpu.VMEM)
     V = pltpu.VMEM
     scratch = [
         V((D, 1536), BF), V((D, D), BF), V((D, 1536), BF), V((D, D), BF), V((D, FF), BF),
         V((FF, D), BF),
         V((1536, D), BF), V((D, D), BF), V((1536, D), BF), V((D, D), BF), V((FF, D), BF),
-        V((D, N), F32), V((D, N), F32), V((D, N), F32),
+        V((D, N), F32), V((D, N), F32), V((D, N), F32), V((3, 1, D), F32),
         V((16, 16, 2, D), BF), V((16, 16, 2, D), BF),
         V((2, 16, 16, D), BF), V((2, 16, 16, D), BF),
         V((2, 16, 16, D), BF), V((2, 16, 16, D), BF),
@@ -316,7 +329,7 @@
         V((1536, N), BF), V((FF, N), BF),
         V((2, HEADS, N, N), BF), V((HEADS, N, N), BF),
         V((2, HEADS, 1, N), F32), V((HEADS, 1, N), F32),
-        pltpu.SemaphoreType.DMA((2,)),
+        pltpu.SemaphoreType.DMA((5,)),
         pltpu.SemaphoreType.DMA((6,)),
         pltpu.SemaphoreType.DMA((N_EX,)),
         pltpu.SemaphoreType.DMA((N_EX,)),
@@ -324,8 +337,7 @@
     res = pl.pallas_call(
         kernel,
         out_shape=jax.ShapeDtypeStruct((16, 2, 16, D), BF),
-        in_specs=[any_spec, any_spec, vm, any_spec, any_spec, vm, any_spec, any_spec, vm,
-                  any_spec, any_spec],
+        in_specs=[any_spec] * 11,
         out_specs=any_spec,
         scratch_shapes=scratch,
         compiler_params=pltpu.CompilerParams(

time: 90.5 us -> 85.7 us (0.947)
  Pallas kernels: 87.9 us -> 83.2 us
    pallas_call x1, Pallas kernels: 87.9 us -> 83.2 us  [local(): pl.pallas_call(kernel, out_shape=jax.ShapeDtypeStruct((16, 2, 16, D), BF)...]
where the time goes in v4:
time: 85.7 us; the launch traced here: 85.6 us
  Pallas kernels  83.2 us (97%)
  local copies, waits for them, and re-layouts  2.38 us (3%)
    pallas_call x1, Pallas kernels, local(): pl.pallas_call(kernel, out_shape=jax.ShapeDtypeStruct((16, 2, 16, D), BF)...  83.2 us
    transpose x1, local copies, waits for them, and re-layouts, local(): return jnp.transpose(res, (2, 0, 1, 3))  2.38 us

profile of v4, /device:TPU:1, one launch (start us, length us, event | category | flops | bytes accessed | tf_op | source)
XLA Modules:
  0.0 85.6 jit_solution(9992171948780334787)
XLA Ops:
  0.0 83.2 %axial_grad.1 = bf16[16,2,16,512]{3,2,1,0:T(8,128)(2,1)} custom-call(bf16[16,16,2,512]{3,2,1,0:T(2,128)(2,1)} %tok.1, bf16[16,16,2,512]{3,2,1,0:T(2,128)(2,1)} %cot.1, f32[1,512]{1,0:T(1,128)} %bitcast.5, bf16[512,1536]{1,0:T(8,128)(2,1)} %wqx.1, bf16[512,512]{1,0:T(8,128)(2,1)} %wox.1, f32[1,512]{1,0:T(1,128)} %bitcast.6, bf16[512,1536]{1,0:T(8,128)(2,1)} %wqy.1, ...), custom_call_target="tpu_custom_call" | custom-call | tf_op jit(solution)/shard_map/axial_grad/pallas_call | solution.py:337
  83.2 2.4 %copy.12 = bf16[16,16,2,512]{3,2,1,0:T(2,128)(2,1)} copy(bf16[16,16,2,512]{3,0,2,1:T(8,128)(2,1)} %bitcast.4) | data formatting | bytes 1048576 | tf_op jit(solution)/shard_map/transpose | solution.py:351

commit v5 on v4

--- a/solution.py
+++ b/solution.py
@@ -46,9 +46,9 @@
 
 def gelu_slope(x):
     k = 0.7978845608028654
-    x2 = x * x
-    t = jnp.tanh(k * x * (1.0 + 0.044715 * x2))
-    return 0.5 * (1.0 + t) + (0.5 * k) * x * (1.0 - t * t) * (1.0 + 0.134145 * x2)
+    p = (6 * 0.044715 * k) * (x * x)
+    a = 0.5 + 0.5 * jnp.tanh(x * (p * (1.0 / 6.0) + k))
+    return a + a * (1.0 - a) * (x * (p + 2.0 * k))
 
 
 def kernel(
@@ -58,7 +58,7 @@
     wqx_t, wox_t, wqy_t, woy_t, wup_t,
     gx_t, gy_t, gm_t, gain_v,
     raw_t, raw_c, tokr, cotr, xl, cl, s1r, yl, g1r, g1x, gtx,
-    xt, s1t, s2t, g2t, ct, ga, qkvx, qkvy, mixx, mixy, nrm, gmx, gqkv, gpre, ex, ey, ix, iy,
+    xt, s1t, s2t, g2t, ct, ga, qkvx, qkvy, mixx, mixy, nrm, gmx, gqkv, gpre, ex, ey, ix, iy, sc, dsb, dlt,
     rsem_raw, wsem, ssem, rsem,
 ):
     gx = lax.axis_index("gx")
@@ -207,34 +207,37 @@
         qkv[...] = nn(wq_t[...], nrm[...]).astype(BF)
         for h in range(HEADS):
             o = h * HD
-            q = qkv[o : o + HD, :] * 0.125
-            k = qkv[o + D : o + D + HD, :]
+            sc[h] = tn(qkv[o + D : o + D + HD, :], qkv[o : o + HD, :] * 0.125)
+        for h in range(HEADS):
+            for t in (0, 128):
+                s = sc[h, :, t : t + 128]
+                e = jnp.exp(s - jnp.max(s, 0, keepdims=True))
+                invs[h, :, t : t + 128] = 1.0 / jnp.sum(e, 0, keepdims=True)
+                es[h, :, t : t + 128] = e.astype(BF)
+        for h in range(HEADS):
+            o = h * HD
             v = qkv[o + 2 * D : o + 2 * D + HD, :]
-            s = tn(k, q)
-            e = jnp.exp(s - jnp.max(s, 0, keepdims=True))
-            inv = 1.0 / jnp.sum(e, 0, keepdims=True)
-            e = e.astype(BF)
-            es[h] = e
-            invs[h] = inv
-            mix[o : o + HD, :] = (nn(v, e) * inv).astype(BF)
+            mix[o : o + HD, :] = (nn(v, es[h]) * invs[h]).astype(BF)
         dst_t[...] = (src_t[...].astype(F32) + nn(wo_t[...], mix[...])).astype(BF)
 
     def heads_back(qkv, es, invs, mix, grad_t, wo):
         gmx[...] = nn(wo[...], grad_t[...]).astype(BF)
         for h in range(HEADS):
             o = h * HD
-            q = qkv[o : o + HD, :]
-            k = qkv[o + D : o + D + HD, :]
-            v = qkv[o + 2 * D : o + 2 * D + HD, :]
-            inv = invs[h]
-            gi = gmx[o : o + HD, :].astype(F32) * inv
-            delta = jnp.sum(gi * mix[o : o + HD, :].astype(F32), 0, keepdims=True)
+            gi = gmx[o : o + HD, :].astype(F32) * invs[h]
+            dlt[h] = jnp.sum(gi * mix[o : o + HD, :].astype(F32), 0, keepdims=True)
             gi = gi.astype(BF)
-            e = es[h]
-            ds = (e.astype(F32) * (tn(v, gi) - delta)).astype(BF)
-            gqkv[o : o + HD, :] = (nn(k, ds) * 0.125).astype(BF)
-            gqkv[o + D : o + D + HD, :] = (nt(q, ds) * 0.125).astype(BF)
-            gqkv[o + 2 * D : o + 2 * D + HD, :] = nt(gi, e).astype(BF)
+            gmx[o : o + HD, :] = gi
+            sc[h] = tn(qkv[o + 2 * D : o + 2 * D + HD, :], gi)
+        for h in range(HEADS):
+            o = h * HD
+            gqkv[o + 2 * D : o + 2 * D + HD, :] = nt(gmx[o : o + HD, :], es[h]).astype(BF)
+        for h in range(HEADS):
+            dsb[h] = (es[h].astype(F32) * (sc[h] - dlt[h])).astype(BF)
+        for h in range(HEADS):
+            o = h * HD
+            gqkv[o : o + HD, :] = (nn(qkv[o + D : o + D + HD, :], dsb[h]) * 0.125).astype(BF)
+            gqkv[o + D : o + D + HD, :] = (nt(qkv[o : o + HD, :], dsb[h]) * 0.125).astype(BF)
 
     def finish_back(src_t, grad_t, gain_t, wq):
         e = nn(wq[...], gqkv[...])
@@ -329,6 +332,7 @@
         V((1536, N), BF), V((FF, N), BF),
         V((2, HEADS, N, N), BF), V((HEADS, N, N), BF),
         V((2, HEADS, 1, N), F32), V((HEADS, 1, N), F32),
+        V((HEADS, N, N), F32), V((HEADS, N, N), BF), V((HEADS, 1, N), F32),
         pltpu.SemaphoreType.DMA((5,)),
         pltpu.SemaphoreType.DMA((6,)),
         pltpu.SemaphoreType.DMA((N_EX,)),

time: 85.7 us -> 82.5 us (0.963)
  Pallas kernels: 83.2 us -> 80 us
    pallas_call x1, Pallas kernels: 83.2 us -> 80 us  [local(): pl.pallas_call(kernel, out_shape=jax.ShapeDtypeStruct((16, 2, 16, D), BF)...]
where the time goes in v5:
time: 82.5 us; the launch traced here: 82.4 us
  Pallas kernels  80 us (97%)
  local copies, waits for them, and re-layouts  2.38 us (3%)
    pallas_call x1, Pallas kernels, local(): pl.pallas_call(kernel, out_shape=jax.ShapeDtypeStruct((16, 2, 16, D), BF)...  80 us
    transpose x1, local copies, waits for them, and re-layouts, local(): return jnp.transpose(res, (2, 0, 1, 3))  2.38 us

profile of v5, /device:TPU:1, one launch (start us, length us, event | category | flops | bytes accessed | tf_op | source)
XLA Modules:
  0.0 82.4 jit_solution(16972611427520147919)
XLA Ops:
  0.0 80.0 %axial_grad.1 = bf16[16,2,16,512]{3,2,1,0:T(8,128)(2,1)} custom-call(bf16[16,16,2,512]{3,2,1,0:T(2,128)(2,1)} %tok.1, bf16[16,16,2,512]{3,2,1,0:T(2,128)(2,1)} %cot.1, f32[1,512]{1,0:T(1,128)} %bitcast.5, bf16[512,1536]{1,0:T(8,128)(2,1)} %wqx.1, bf16[512,512]{1,0:T(8,128)(2,1)} %wox.1, f32[1,512]{1,0:T(1,128)} %bitcast.6, bf16[512,1536]{1,0:T(8,128)(2,1)} %wqy.1, ...), custom_call_target="tpu_custom_call" | custom-call | tf_op jit(solution)/shard_map/axial_grad/pallas_call | solution.py:341
  80.0 2.4 %copy.12 = bf16[16,16,2,512]{3,2,1,0:T(2,128)(2,1)} copy(bf16[16,16,2,512]{3,0,2,1:T(8,128)(2,1)} %bitcast.4) | data formatting | bytes 1048576 | tf_op jit(solution)/shard_map/transpose | solution.py:355

commit v6 on v5

--- a/solution.py
+++ b/solution.py
@@ -286,14 +286,14 @@
         send_out(c)
 
     x_fwd(0)
+    x_fwd(1)
     send_cot(1)
-    x_fwd(1)
     y_act(0)
-    y_act(1)
     y_fwd(0)
     y_mlp(0)
     y_bwd(0)
     y_fwd(1)
+    y_act(1)
     y_mlp(1)
     y_bwd(1)
     x_bwd(0)

time: 82.5 us -> 80.5 us (0.976)
  Pallas kernels: 80 us -> 78 us
    pallas_call x1, Pallas kernels: 80 us -> 78 us  [local(): pl.pallas_call(kernel, out_shape=jax.ShapeDtypeStruct((16, 2, 16, D), BF)...]
where the time goes in v6:
time: 80.5 us; the launch traced here: 80.4 us
  Pallas kernels  78 us (97%)
  local copies, waits for them, and re-layouts  2.38 us (3%)
    pallas_call x1, Pallas kernels, local(): pl.pallas_call(kernel, out_shape=jax.ShapeDtypeStruct((16, 2, 16, D), BF)...  78 us
    transpose x1, local copies, waits for them, and re-layouts, local(): return jnp.transpose(res, (2, 0, 1, 3))  2.38 us

profile of v6, /device:TPU:1, one launch (start us, length us, event | category | flops | bytes accessed | tf_op | source)
XLA Modules:
  0.0 80.4 jit_solution(4686504477594852929)
XLA Ops:
  0.0 78.0 %axial_grad.1 = bf16[16,2,16,512]{3,2,1,0:T(8,128)(2,1)} custom-call(bf16[16,16,2,512]{3,2,1,0:T(2,128)(2,1)} %tok.1, bf16[16,16,2,512]{3,2,1,0:T(2,128)(2,1)} %cot.1, f32[1,512]{1,0:T(1,128)} %bitcast.5, bf16[512,1536]{1,0:T(8,128)(2,1)} %wqx.1, bf16[512,512]{1,0:T(8,128)(2,1)} %wox.1, f32[1,512]{1,0:T(1,128)} %bitcast.6, bf16[512,1536]{1,0:T(8,128)(2,1)} %wqy.1, ...), custom_call_target="tpu_custom_call" | custom-call | tf_op jit(solution)/shard_map/axial_grad/pallas_call | solution.py:341
  78.1 2.4 %copy.12 = bf16[16,16,2,512]{3,2,1,0:T(2,128)(2,1)} copy(bf16[16,16,2,512]{3,0,2,1:T(8,128)(2,1)} %bitcast.4) | data formatting | bytes 1048576 | tf_op jit(solution)/shard_map/transpose | solution.py:355
